TPU v7x, 768 devices: a whole 4x8x12 slice. The times are simulated.
768 devices in a mesh: grp: 4 (over x), blk: 192 (over z, y, core).
Axes of the slice: x: 4, y: 8, z: 12, core: 2. Of those that a mesh axis runs over, the one named last changes fastest.
Arguments:
- edge_state: bfloat16 [294912, 512], P(('grp', 'blk')), may hold values from -6 to 6
- basis: bfloat16 [18432, 16, 16], P(('grp', 'blk')), may hold values from -1.5 to 1.5
- weights: bfloat16 [3, 512, 512], replicated, may hold values from -0.25 to 0.25
- partner: int32 [2304], P(('grp', 'blk')), may hold values from 0 to 11, as said below
- cotangent: bfloat16 [294912, 512], P(('grp', 'blk')), may hold values from -6 to 6
Outputs:
- edge_out: bfloat16 [294912, 512], P(('grp', 'blk'))
- grad_state: bfloat16 [294912, 512], P(('grp', 'blk'))
- weight_grad: float32 [1536, 512], P(('grp', 'blk'))
Inputs may be any that keep to these rules, and one draw needn't show every extreme that they name: partner pairs the blocks of each group: partner[partner[k]] = k within the group, and a block may be its own partner. A device pairs at most 1 of its blocks with blocks of any one other device of its group, and exactly 1 with those of one of them.
All inputs are finite; a program needn't handle non-finite values.
Results may differ from a plain program's by a relative error of at most 0.008.
Values may be sent and summed in bfloat16 or wider, within the bound.
No kernel may reach another device: no remote copies, remote signals or barrier semaphores. Data moves between devices by JAX's collectives and lax.ppermute only.
A program may use at most 32 MiB of HBM per device.

v0:
```python
import math

import jax
import jax.numpy as jnp
from jax import lax
from jax.sharding import Mesh
from jax.sharding import PartitionSpec as P

NBR = 16
CAP = 1
BLK = ("blk_0", "blk_1", "blk_2")
GRP_BLK = ("grp", "blk_0", "blk_1", "blk_2")


def split_up(shard, dim, length):
    dims = shard.shape
    tiles = shard.reshape(*dims[:dim], length, dims[dim] // length, *dims[dim + 1 :])
    return jnp.moveaxis(tiles, dim, 0)


def summed_on_arrival(shard, axis, dim):
    tiles = split_up(shard, dim, lax.axis_size(axis))
    arrived = lax.all_to_all(tiles, axis, split_axis=0, concat_axis=0, tiled=True)
    return arrived.astype(jnp.float32).sum(axis=0)


def reduced_to_own(tiles, axes, sequence):
    dims = [lax.axis_size(a) for a in axes]
    tiles = tiles.reshape(*dims, *tiles.shape[1:])
    tiles = tiles.transpose(*sequence, *range(len(axes), tiles.ndim))
    tiles = tiles.reshape(-1, *tiles.shape[len(axes) :])
    for k in sequence:
        tiles = lax.psum_scatter(tiles, axes[k], scatter_dimension=0, tiled=True)
    return tiles[0]


def scatter_axes(shard, axes, sequence, dim):
    length = lax.axis_size(axes)
    return reduced_to_own(split_up(shard, dim, length), axes, sequence)


def norm_rows(hidden):
    return hidden * lax.rsqrt(jnp.mean(hidden * hidden, axis=-1, keepdims=True) + 1e-06)


def layer_forward(hidden, weight):
    normed = norm_rows(hidden).astype(jnp.bfloat16)
    preact = jnp.dot(normed, weight, preferred_element_type=jnp.float32)
    return (hidden + jax.nn.silu(preact), normed, preact)


def layer_backward(hidden, normed, preact, weight, upstream):
    sigma = jax.nn.sigmoid(preact)
    grad_pre = (upstream * sigma * (1.0 + preact * (1.0 - sigma))).astype(jnp.bfloat16)
    grad_weight = lax.dot_general(
        normed, grad_pre, (((0,), (0,)), ((), ())), preferred_element_type=jnp.float32
    )
    grad_normed = lax.dot_general(
        grad_pre, weight, (((1,), (1,)), ((), ())), preferred_element_type=jnp.float32
    )
    inverse = lax.rsqrt(jnp.mean(hidden * hidden, axis=-1, keepdims=True) + 1e-06)
    unit = hidden * inverse
    inner = jnp.mean(grad_normed * unit, axis=-1, keepdims=True)
    return (upstream + inverse * (grad_normed - unit * inner), grad_weight)


def flip_rows(blocks):
    count, height, width = blocks.shape
    return blocks.reshape(count, height // 2, 2, width)[:, :, ::-1, :].reshape(count, height, width)


def route_plan(partner, own_index, group_count):
    block_count = partner.shape[0]
    target = partner // block_count
    remote = partner % block_count
    order = jnp.arange(block_count)
    same = target[:, None] == target[None, :]
    send_rank = jnp.sum(same & (order[None, :] < order[:, None]), axis=1)
    recv_rank = jnp.sum(same & (remote[None, :] < remote[:, None]), axis=1)
    local_pair = target == own_index
    slots = jnp.arange(group_count * CAP)
    send_slot = target * CAP + send_rank
    recv_slot = target * CAP + recv_rank
    pack_matrix = ((slots[:, None] == send_slot[None, :]) & ~local_pair[None, :]).astype(
        jnp.bfloat16
    )
    unpack_matrix = ((recv_slot[:, None] == slots[None, :]) & ~local_pair[:, None]).astype(
        jnp.bfloat16
    )
    return (pack_matrix, unpack_matrix, local_pair)


def pack_blocks(values, pack_matrix, block_count):
    blocks = values.reshape(block_count, -1, values.shape[1])
    return jnp.einsum("sn,nrd->srd", pack_matrix, blocks, preferred_element_type=jnp.bfloat16)


def unpack_blocks(arrived, unpack_matrix, local_pair, values, block_count):
    blocks = values.reshape(block_count, -1, values.shape[1])
    distant = jnp.einsum("ns,srd->nrd", unpack_matrix, arrived, preferred_element_type=jnp.bfloat16)
    joined = jnp.where(local_pair[:, None, None], blocks, distant)
    return flip_rows(joined).reshape(values.shape)


def local(edge_state, basis, weights, partner, cotangent):
    row_count, width = edge_state.shape
    block_count = partner.shape[0]
    group_count = lax.axis_size("grp")
    own_index = lax.axis_index("grp")
    total_edges = row_count * group_count * lax.axis_size(BLK)
    pack_matrix, unpack_matrix, local_pair = route_plan(partner, own_index, group_count)
    mixed = jnp.einsum(
        "aij,ajd->aid",
        basis,
        edge_state.reshape(-1, NBR, width),
        preferred_element_type=jnp.float32,
    ).reshape(row_count, width)
    first, normed_one, pre_one = layer_forward(mixed, weights[0])
    second, normed_two, pre_two = layer_forward(first, weights[1])
    sent = second.astype(jnp.bfloat16)
    arrived = lax.all_to_all(
        pack_blocks(sent, pack_matrix, block_count), "grp", split_axis=0, concat_axis=0, tiled=True
    )
    reversed_state = unpack_blocks(arrived, unpack_matrix, local_pair, sent, block_count)
    summed = second + reversed_state.astype(jnp.float32)
    final, normed_three, pre_three = layer_forward(summed, weights[2])
    edge_out = final.astype(jnp.bfloat16)
    grad_summed, grad_three = layer_backward(
        summed, normed_three, pre_three, weights[2], cotangent.astype(jnp.float32)
    )
    grad_reversed = grad_summed.astype(jnp.bfloat16)
    returned = lax.all_to_all(
        pack_blocks(grad_reversed, pack_matrix, block_count),
        "grp",
        split_axis=0,
        concat_axis=0,
        tiled=True,
    )
    grad_sent = unpack_blocks(returned, unpack_matrix, local_pair, grad_reversed, block_count)
    grad_second = grad_summed + grad_sent.astype(jnp.float32)
    grad_first, grad_two = layer_backward(first, normed_two, pre_two, weights[1], grad_second)
    grad_mixed, grad_one = layer_backward(mixed, normed_one, pre_one, weights[0], grad_first)
    grad_round = grad_mixed.astype(jnp.bfloat16).reshape(-1, NBR, width)
    grad_state = (
        jnp.einsum("aij,aid->ajd", basis, grad_round, preferred_element_type=jnp.float32)
        .reshape(row_count, width)
        .astype(jnp.bfloat16)
    )
    local_grads = jnp.concatenate([grad_one, grad_two, grad_three], axis=0)
    group_part = summed_on_arrival(local_grads.astype(jnp.bfloat16), "grp", 0)
    summed_grads = scatter_axes(group_part, BLK, (2, 0, 1), 0)
    weight_grad = summed_grads * (1.0 / math.sqrt(total_edges))
    return (edge_out, grad_state, weight_grad)


def solution(mesh):
    split = Mesh(
        mesh.devices.reshape(mesh.shape["grp"], 12, 8, 2), ("grp", "blk_0", "blk_1", "blk_2")
    )
    return jax.shard_map(
        local,
        mesh=split,
        in_specs=(P(GRP_BLK, None), P(GRP_BLK, None, None), P(), P(GRP_BLK), P(GRP_BLK, None)),
        out_specs=(P(GRP_BLK, None), P(GRP_BLK, None), P(GRP_BLK, None)),
        check_vma=False,
    )
```

profile of v0, /device:TPU:2, one launch (start us, length us, event | category | flops | bytes accessed | tf_op | source)
XLA Modules:
  0.0 217.1 jit_solution(2951716828657426127)
XLA Ops:
  7.2 1.0 copy.54
  8.9 2.4 %multiply_reduce_fusion.4 = (f32[384]{0:T(512)S(1)}, f32[384,512]{1,0:T(8,128)S(1)}, f32[384,512]{1,0:T(8,128)}) fusion(f32[24,16,512]{2,1,0:T(8,128)S(1)} %get-tuple-element.22, bf16[384,512]{1,0:T(8,128)(2,1)S(1)} %bitcast.83, bf16[3,512,512]{2,1,0:T(8,128)(2,1)} %param.7), kind=kOutput, calls=%fused_computation.26 | convolution fusion | flops 202702464 | bytes 3278336 | tf_op jit(solution)/shard_map/dot_general | solution.py:48
  11.4 1.6 fusion.37
  13.8 18.5 %all_to_all.15 = bf16[4,128,512]{2,1,0:T(8,128)(2,1)S(1)} all-to-all(bf16[4,128,512]{2,1,0:T(8,128)(2,1)S(1)} %copy.45), channel_id=1, replica_groups=mesh['grp'=4,'blk_0'=12,'blk_1'=8,'blk_2'=2] {'grp'}, dimensions={0} | all-to-all | bytes 1048576 | tf_op jit(solution)/shard_map/all_to_all | solution.py:121
  33.5 3.6 %rev.6 = bf16[3,64,2,512]{3,2,1,0:T(2,128)(2,1)S(1)} reverse(bf16[3,64,2,512]{3,2,1,0:T(2,128)(2,1)S(1)} %copy.48), dimensions={2} | reverse | bytes 786432 | tf_op jit(solution)/shard_map/rev | solution.py:69
  37.1 1.0 reshape.113
  38.1 1.6 multiply_reduce_fusion.3
  39.8 1.4 fusion.1
  44.6 5.6 %all-to-all-start.1 = ((bf16[4,128,512]{2,1,0:T(8,128)(2,1)}), bf16[4,128,512]{2,1,0:T(8,128)(2,1)}, u32[]{:S(2)}, u32[]{:S(2)}) async-start(bf16[4,128,512]{2,1,0:T(8,128)(2,1)} %copy.50), calls=%async_computation.1 | async-start | bytes 1048576 | tf_op jit(solution)/shard_map/all_to_all | solution.py:132
  50.9 2.3 %convolution_convert_fusion = bf16[512,512]{1,0:T(8,128)(2,1)} fusion(bf16[384,512]{1,0:T(8,128)(2,1)} %copy-done.6, f32[384,512]{1,0:T(8,128)S(1)} %get-tuple-element.10, f32[384]{0:T(512)S(1)} %add_rsqrt_fusion.1), kind=kOutput, calls=%fused_computation.2 | convolution fusion | flops 201981952 | bytes 1705472 | tf_op jit(solution)/shard_map/dot_general | solution.py:55
  53.2 3.7 %all-to-all-done.1 = bf16[4,128,512]{2,1,0:T(8,128)(2,1)} async-done(((bf16[4,128,512]{2,1,0:T(8,128)(2,1)}), bf16[4,128,512]{2,1,0:T(8,128)(2,1)}, u32[]{:S(2)}, u32[]{:S(2)}) %all-to-all-start.1) | async-done | bytes 524320 | tf_op jit(solution)/shard_map/all_to_all | solution.py:132
  56.9 1.9 convolution_select_fusion
  58.8 1.1 copy.53
  59.9 5.4 %rev.7 = bf16[3,64,2,512]{3,2,1,0:T(2,128)(2,1)} reverse(bf16[3,64,2,512]{3,2,1,0:T(2,128)(2,1)} %copy.53), dimensions={2} | reverse | bytes 786432 | tf_op jit(solution)/shard_map/rev | solution.py:69
  65.4 2.0 reshape.114
  67.4 3.2 %multiply_convert_fusion.1 = (bf16[384,512]{1,0:T(8,128)(2,1)S(1)}, f32[384,512]{1,0:T(8,128)S(1)}, bf16[384,512]{1,0:T(8,128)(2,1)}) fusion(f32[384,512]{1,0:T(8,128)} %copy-done.1, f32[384,512]{1,0:T(8,128)} %reshape.114, f32[384,512]{1,0:T(8,128)S(1)} %get-tuple-element.29, f32[384]{0:T(512)S(1)} %copy-done.14, f32[384,512]{1,0:T(8,128)S(1)} %get-tuple-element.10, ...), kind=kLoop, calls=%fused_computation.19 | loop fusion | flops 4325376 | bytes 5901312 | tf_op jit(solution)/shard_map/convert_element_type | solution.py:54
  74.0 16.1 %all_to_all.16 = bf16[4,384,512]{2,1,0:T(8,128)(2,1)S(1)} all-to-all(bf16[4,384,512]{2,1,0:T(8,128)(2,1)S(1)} %bitcast.74), channel_id=1, replica_groups=mesh['grp'=4,'blk_0'=12,'blk_1'=8,'blk_2'=2] {'grp'}, dimensions={0} | all-to-all | bytes 3145728 | tf_op jit(solution)/shard_map/all_to_all | solution.py:23
  90.9 1.1 copy.55
  92.1 24.5 %reduce-scatter.3.cloned.1.call-done = f32[96,2,512]{2,0,1:T(8,128)} async-done(((f32[192,2,512]{2,0,1:T(8,128)}), f32[96,2,512]{2,0,1:T(8,128)}) %reduce-scatter.3.cloned.1.call-update) | async-done | bytes 393232 | tf_op jit(solution)/shard_map/reduce_scatter | solution.py:33
  116.6 1.3 dynamic-slice
  117.9 1.0 convolution_convert_fusion.3
  118.9 59.7 %reduce-scatter.5.cloned.1.call-done = f32[8,2,512]{2,0,1:T(8,128)} async-done(((f32[96,2,512]{2,0,1:T(8,128)}), f32[8,2,512]{2,0,1:T(8,128)}) %reduce-scatter.5.cloned.1.call-update) | async-done | bytes 32784 | tf_op jit(solution)/shard_map/reduce_scatter | solution.py:33
  179.4 29.7 %all-reduce = f32[8,2,512]{2,1,0:T(2,128)S(1)} all-reduce(f32[8,2,512]{2,1,0:T(2,128)S(1)} %copy.56), channel_id=4, replica_groups=mesh['grp'=4,'blk_0'=12,'blk_1'=8,'blk_2'=2] {'blk_1'}, use_global_device_ids=true, to_apply=%region_11.12.clone | all-reduce | flops 8192 | bytes 65536
  209.0 1.2 fusion.27
  (81 shorter events, 11.7 us)
Async XLA Ops:
  7.2 1.1 copy-start
  8.9 2.5 %copy-start.16 = (s32[3]{0:T(128)S(1)}, s32[3]{0:T(128)}, u32[]{:S(2)}) copy-start(s32[3]{0:T(128)} %param.8) | copy-start | bytes 40
  11.3 1.7 copy-start.11
  11.4 21.0 %copy-start.17 = (pred[3]{0:T(512)(128)(4,1)}, pred[3]{0:T(512)(128)(4,1)S(1)}, u32[]{:S(2)}) copy-start(pred[3]{0:T(512)(128)(4,1)S(1)} %get-tuple-element.11) | copy-start | bytes 13
  11.4 21.0 %copy-start.19 = (pred[3]{0:T(512)(128)(4,1)}, pred[3]{0:T(512)(128)(4,1)S(1)}, u32[]{:S(2)}) copy-start(pred[3]{0:T(512)(128)(4,1)S(1)} %get-tuple-element.12) | copy-start | bytes 13
  13.0 25.1 %copy-start.1 = (f32[384,512]{1,0:T(8,128)}, f32[384,512]{1,0:T(8,128)S(1)}, u32[]{:S(2)}) copy-start(f32[384,512]{1,0:T(8,128)S(1)} %get-tuple-element.25) | copy-start | bytes 2359300
  13.2 19.1 %copy-start.21 = (s32[3]{0:T(128)}, s32[3]{0:T(128)S(1)}, u32[]{:S(2)}) copy-start(s32[3]{0:T(128)S(1)} %get-tuple-element.20) | copy-start | bytes 40
  13.2 19.1 %copy-start.20 = (s32[3]{0:T(128)}, s32[3]{0:T(128)S(1)}, u32[]{:S(2)}) copy-start(s32[3]{0:T(128)S(1)} %get-tuple-element.19) | copy-start | bytes 40
  38.1 1.7 copy-start.3
  38.1 1.7 copy-start.5
  41.2 0.7 copy-start.6
  42.0 1.3 copy-start.18
  42.0 1.3 copy-start.22
  42.5 0.7 copy-start.10
  44.6 12.3 %all-to-all-start.1 = ((bf16[4,128,512]{2,1,0:T(8,128)(2,1)}), bf16[4,128,512]{2,1,0:T(8,128)(2,1)}, u32[]{:S(2)}, u32[]{:S(2)}) async-start(bf16[4,128,512]{2,1,0:T(8,128)(2,1)} %copy.50), calls=%async_computation.1 | async-start | bytes 1048576 | tf_op jit(solution)/shard_map/all_to_all | solution.py:132
  50.2 66.4 %reduce-scatter.3.cloned.1.call-start = ((), (), s32[]{:S(2)}) async-start(), calls=%async_computation.5 | async-start | bytes 1179648 | tf_op jit(solution)/shard_map/reduce_scatter | solution.py:33
  58.8 8.5 %copy-start.14 = (f32[384]{0:T(512)S(1)}, f32[384]{0:T(512)}, u32[]{:S(2)}) copy-start(f32[384]{0:T(512)} %copy-done.13) | copy-start | bytes 4612
  67.4 3.2 %copy-start.4 = (bf16[3,512,512]{2,1,0:T(8,128)(2,1)S(1)}, bf16[3,512,512]{2,1,0:T(8,128)(2,1)}, u32[]{:S(2)}) copy-start(bf16[3,512,512]{2,1,0:T(8,128)(2,1)} %param.7) | copy-start | bytes 4718596
  67.4 3.2 %copy-start.12 = (f32[384]{0:T(512)S(1)}, f32[384]{0:T(512)}, u32[]{:S(2)}) copy-start(f32[384]{0:T(512)} %copy-done.11) | copy-start | bytes 4612
  70.6 1.1 copy-start.9
  71.7 0.7 copy-start.15
  72.9 1.0 copy-start.2
  90.9 27.0 %copy-start.8 = (bf16[24,16,16]{1,2,0:T(8,128)(2,1)S(1)}, bf16[24,16,16]{1,2,0:T(8,128)(2,1)}, u32[]{:S(2)}) copy-start(bf16[24,16,16]{1,2,0:T(8,128)(2,1)} %copy-done.7) | copy-start | bytes 36868
  92.1 86.5 %reduce-scatter.5.cloned.1.call-start = ((), (), s32[]{:S(2)}) async-start(), calls=%async_computation.6 | async-start | bytes 425984 | tf_op jit(solution)/shard_map/reduce_scatter | solution.py:33
  (2 other events, 1.2 us)
Sparse Core Ops, SparseCore 0:
  92.2 24.3 reduce-scatter.2
  119.7 58.8 reduce-scatter.4
where the time goes:
time: 218 us; the launch traced here: 217 us
  waiting for transfers between devices  87.9 us (40%)
  blocking collectives  64.3 us (29%)
  local copies, waits for them, and re-layouts  22 us (10%)
  matrix products  15.2 us (7%)
  between operations  14.3 us (7%)
  other arithmetic  7.78 us (4%)
  starting transfers between devices  5.6 us (3%)
    reduce_scatter x2, waiting for transfers between devices, reduced_to_own(): tiles = lax.psum_scatter(tiles, axes[k], scatter_dimension=0, tiled=True)  84.2 us
    unnamed x1, blocking collectives  29.7 us
    all_to_all x1, blocking collectives, local(): lax.all_to_all(pack_blocks(sent, pack_matrix, block_count), 'grp', split_...  18.5 us
    all_to_all x1, blocking collectives, summed_on_arrival(): lax.all_to_all(tiles, axis, split_axis=0, concat_axis=0, tiled=True)  16.1 us
    rev x2, local copies, waits for them, and re-layouts, flip_rows(): blocks.reshape(count, height // 2, 2, width)[:, :, ::-1, :]  9.02 us
    all_to_all x1, starting transfers between devices, local(): lax.all_to_all(pack_blocks(grad_reversed, pack_matrix, block_count), 'grp...  5.56 us
    dot_general x3, matrix products, layer_forward(): preact = jnp.dot(normed, weight, preferred_element_type=jnp.float32)  5.45 us
    unnamed x48, local copies, waits for them, and re-layouts  4.51 us
  transfers between devices with their start and end apart: 3, of which 3 were waited for; matrix products, arithmetic and copies ran while one was open for 2% of the time, Pallas kernels for 0%

commit v1 on v0

v1 whole, which is shorter than its diff:
```python
import functools
import math

import jax
import jax.numpy as jnp
import numpy as np
from jax import lax
from jax.experimental import pallas as pl
from jax.experimental.pallas import tpu as pltpu
from jax.sharding import Mesh
from jax.sharding import PartitionSpec as P

NBR = 16
BLOCK = 128
GRP_BLK = ("grp", "blk_0", "blk_1", "blk_2")
BF16 = jnp.bfloat16
F32 = jnp.float32


def dot(a, b):
    return jnp.dot(a, b, preferred_element_type=F32)


def dot_nt(a, b):
    return lax.dot_general(a, b, (((1,), (1,)), ((), ())), preferred_element_type=F32)


def dot_tn(a, b):
    return lax.dot_general(a, b, (((0,), (0,)), ((), ())), preferred_element_type=F32)


def inverse_norm(hidden):
    return lax.rsqrt(jnp.mean(hidden * hidden, axis=-1, keepdims=True) + 1e-06)


def sigmoid(v):
    return 1.0 / (1.0 + jnp.exp(-v))


def layer_backward(unit, inverse, preact, weight, upstream):
    sigma = sigmoid(preact)
    grad_pre = (upstream * sigma * (1.0 + preact * (1.0 - sigma))).astype(BF16)
    grad_normed = dot_nt(grad_pre, weight)
    inner = jnp.mean(grad_normed * unit, axis=-1, keepdims=True)
    return upstream + inverse * (grad_normed - unit * inner), grad_pre


def basis_blocks(basis, count):
    wide_row = lax.broadcasted_iota(jnp.int32, (NBR, BLOCK), 0)
    wide_col = lax.broadcasted_iota(jnp.int32, (NBR, BLOCK), 1)
    spread = jnp.where(wide_col % NBR == wide_row, 1.0, 0.0).astype(BF16)
    tiled = dot(basis, spread)
    row = lax.broadcasted_iota(jnp.int32, (BLOCK, BLOCK), 0)
    col = lax.broadcasted_iota(jnp.int32, (BLOCK, BLOCK), 1)
    same = row // NBR == col // NBR
    return [
        jnp.where(same, tiled[n * BLOCK : (n + 1) * BLOCK], 0.0).astype(BF16) for n in range(count)
    ]


def owner_of(number, count):
    owner = jnp.int32(0)
    for edge in range(1, 4):
        owner = owner + (number >= edge * count).astype(jnp.int32)
    return owner


def fill_slots(slots_ref, blocks_ref, partner_ref, group_count, count):
    owners = [owner_of(partner_ref[n], count) for n in range(count)]
    for d in range(group_count):
        pick = jnp.int32(0)
        for n in range(1, count):
            pick = jnp.where(owners[n] == d, n, pick)
        start = pl.multiple_of(pick * BLOCK, BLOCK)
        slots_ref[d] = blocks_ref[pl.ds(start, BLOCK), :]


def reverse_blocks(arrived_ref, own_ref, partner_ref, index_ref, count):
    row = lax.broadcasted_iota(jnp.int32, (BLOCK, BLOCK), 0)
    col = lax.broadcasted_iota(jnp.int32, (BLOCK, BLOCK), 1)
    flip = jnp.where(row + 1 - 2 * (row % 2) == col, 1.0, 0.0).astype(BF16)
    picked = []
    for n in range(count):
        number = partner_ref[n]
        owner = owner_of(number, count)
        start = pl.multiple_of((number - owner * count) * BLOCK, BLOCK)
        near = own_ref[pl.ds(start, BLOCK), :].astype(BF16)
        picked.append(dot(flip, jnp.where(owner == index_ref[0], near, arrived_ref[owner])))
    return jnp.concatenate(picked, axis=0)


def forward_body(partner_ref, edge_ref, basis_ref, weight_ref, mixed_ref, pre_one_ref, pre_two_ref,
                 second_ref, slots_ref, sent_ref):
    count = edge_ref.shape[0] // BLOCK
    blocks = basis_blocks(basis_ref[...], count)
    mixed = jnp.concatenate(
        [dot(blocks[n], edge_ref[n * BLOCK : (n + 1) * BLOCK, :]) for n in range(count)], axis=0
    )
    mixed_ref[...] = mixed
    pre_one = dot((mixed * inverse_norm(mixed)).astype(BF16), weight_ref[0])
    pre_one_ref[...] = pre_one
    first = mixed + pre_one * sigmoid(pre_one)
    pre_two = dot((first * inverse_norm(first)).astype(BF16), weight_ref[1])
    pre_two_ref[...] = pre_two
    second = first + pre_two * sigmoid(pre_two)
    second_ref[...] = second
    sent_ref[...] = second.astype(BF16)
    fill_slots(slots_ref, sent_ref, partner_ref, slots_ref.shape[0], count)


def middle_body(partner_ref, index_ref, second_ref, arrived_ref, weight_ref, cotangent_ref,
                edge_out_ref, grad_summed_ref, normed_ref, grad_pre_ref, slots_ref, sent_ref):
    count = second_ref.shape[0] // BLOCK
    summed = second_ref[...] + reverse_blocks(arrived_ref, second_ref, partner_ref, index_ref, count)
    inverse = inverse_norm(summed)
    unit = summed * inverse
    normed = unit.astype(BF16)
    normed_ref[...] = normed
    preact = dot(normed, weight_ref[2])
    edge_out_ref[...] = (summed + preact * sigmoid(preact)).astype(BF16)
    grad_summed, grad_pre = layer_backward(
        unit, inverse, preact, weight_ref[2], cotangent_ref[...].astype(F32)
    )
    grad_pre_ref[...] = grad_pre
    grad_summed_ref[...] = grad_summed
    sent_ref[...] = grad_summed.astype(BF16)
    fill_slots(slots_ref, sent_ref, partner_ref, slots_ref.shape[0], count)


def layer_pieces(layer, groups, deep):
    per_layer = groups * deep // 3
    pieces = []
    done = 0
    while done < per_layer:
        number = per_layer * layer + done
        size = min(per_layer - done, deep - number % deep)
        pieces.append((number // deep, number % deep, done, size))
        done += size
    return pieces


def row_order(groups, deep, high, cores):
    order = []
    for layer in range(3):
        rows = []
        for _, _, done, size in layer_pieces(layer, groups, deep):
            y, z, i = np.meshgrid(np.arange(high), np.arange(size), np.arange(2), indexing="ij")
            rows.append((2 * cores * high * (z + done) + 2 * cores * y + i).reshape(-1))
        rows = np.concatenate(rows)
        order.append(np.concatenate([rows, rows]))
    return np.stack(order).astype(np.int32)


def permuted(normed, order, core):
    width = normed.shape[1]
    place = lax.broadcasted_iota(jnp.int32, (1, width), 1)
    source = order + 2 * jnp.where(place < width // 2, core, 1 - core)
    row = lax.broadcasted_iota(jnp.int32, (width, width), 0)
    choice = jnp.where(row == source, 1.0, 0.0).astype(BF16)
    return dot(normed, choice).astype(BF16)


def spread_rows(wide_ref, grad_weight, layer, high):
    groups, part = wide_ref.shape[1:3]
    deep = part // (2 * high)
    half = grad_weight.shape[0] // 2
    for side in range(2):
        start = side * half
        for g, z, _, size in layer_pieces(layer, groups, deep):
            for y in range(high):
                to = 2 * deep * y + 2 * z
                wide_ref[side, g, to : to + 2 * size, :] = grad_weight[start : start + 2 * size]
                start += 2 * size


def backward_body(partner_ref, index_ref, grad_summed_ref, arrived_ref, mixed_ref, pre_one_ref,
                  pre_two_ref, normed_three_ref, grad_pre_three_ref, weight_ref, basis_ref,
                  order_ref, grad_state_ref, keep_ref, send_ref, wide_ref, *, high):
    count = mixed_ref.shape[0] // BLOCK
    mixed = mixed_ref[...]
    pre_one = pre_one_ref[...]
    pre_two = pre_two_ref[...]
    grad_second = grad_summed_ref[...] + reverse_blocks(
        arrived_ref, grad_summed_ref, partner_ref, index_ref, count
    )
    first = mixed + pre_one * sigmoid(pre_one)
    inverse_two = inverse_norm(first)
    unit_two = first * inverse_two
    grad_first, grad_pre_two = layer_backward(
        unit_two, inverse_two, pre_two, weight_ref[1], grad_second
    )
    inverse_one = inverse_norm(mixed)
    unit_one = mixed * inverse_one
    grad_mixed, grad_pre_one = layer_backward(
        unit_one, inverse_one, pre_one, weight_ref[0], grad_first
    )
    grad_round = grad_mixed.astype(BF16)
    blocks = basis_blocks(basis_ref[...], count)
    for n in range(count):
        rows = slice(n * BLOCK, (n + 1) * BLOCK)
        grad_state_ref[rows, :] = dot_tn(blocks[n], grad_round[rows]).astype(BF16)
    core = index_ref[1]
    pairs = (
        (unit_one.astype(BF16), grad_pre_one),
        (unit_two.astype(BF16), grad_pre_two),
        (normed_three_ref[...], grad_pre_three_ref[...]),
    )
    for layer, (normed, grad_pre) in enumerate(pairs):
        ordered = permuted(normed, order_ref[layer : layer + 1, :], core)
        spread_rows(wide_ref, dot_tn(ordered, grad_pre), layer, high)
    keep_ref[...] = wide_ref[0].astype(BF16)
    send_ref[...] = wide_ref[1].astype(BF16)


def call(body, name, scalars, arrays, outs, scratch):
    smem = pl.BlockSpec(memory_space=pltpu.SMEM)
    vmem = pl.BlockSpec(memory_space=pltpu.VMEM)
    return pl.pallas_call(
        body,
        name=name,
        in_specs=[smem] * len(scalars) + [vmem] * len(arrays),
        out_specs=[vmem] * len(outs),
        out_shape=[jax.ShapeDtypeStruct(*o) for o in outs],
        scratch_shapes=[pltpu.VMEM(*s) for s in scratch],
    )(*scalars, *arrays)


def summed_over(pieces, axis):
    arrived = lax.all_to_all(pieces, axis, split_axis=0, concat_axis=0, tiled=True)
    return arrived.astype(F32).sum(axis=0)


def local(edge_state, basis, weights, partner, cotangent):
    rows, width = edge_state.shape
    groups, deep, high, cores = (lax.axis_size(a) for a in GRP_BLK)
    total_edges = rows * groups * deep * high * cores
    index = jnp.stack([lax.axis_index("grp"), lax.axis_index("blk_2")]).astype(jnp.int32)
    flat_basis = basis.reshape(rows, NBR)
    full = ((rows, width), F32)
    half = ((rows, width), BF16)
    slots = ((groups, BLOCK, width), BF16)
    mixed, pre_one, pre_two, second, sent = call(
        forward_body, "forward", [partner], [edge_state, flat_basis, weights],
        [full, full, full, full, slots], [half],
    )
    arrived = lax.all_to_all(sent, "grp", split_axis=0, concat_axis=0, tiled=True)
    edge_out, grad_summed, normed_three, grad_pre_three, sent_back = call(
        middle_body, "middle", [partner, index], [second, arrived, weights, cotangent],
        [half, full, half, half, slots], [half],
    )
    returned = lax.all_to_all(sent_back, "grp", split_axis=0, concat_axis=0, tiled=True)
    part = 3 * width // (groups * cores)
    pieces = (groups, part, width)
    order = jnp.asarray(row_order(groups, deep, high, cores))
    grad_state, keep, send = call(
        functools.partial(backward_body, high=high), "backward", [partner, index],
        [grad_summed, returned, mixed, pre_one, pre_two, normed_three, grad_pre_three, weights,
         flat_basis, order],
        [half, (pieces, BF16), (pieces, BF16)],
        [((2, *pieces), F32)],
    )
    other = lax.ppermute(send, "blk_2", [(0, 1), (1, 0)])
    pair = (keep.astype(F32) + other.astype(F32)).astype(BF16)
    line = summed_over(pair, "grp").astype(BF16)
    plane = summed_over(line.reshape(high, part // high, width), "blk_1").astype(BF16)
    final = summed_over(plane.reshape(deep, part // high // deep, width), "blk_0")
    return edge_out, grad_state, final * (1.0 / math.sqrt(total_edges))


def solution(mesh):
    split = Mesh(mesh.devices.reshape(mesh.shape["grp"], 12, 8, 2), GRP_BLK)
    return jax.shard_map(
        local,
        mesh=split,
        in_specs=(P(GRP_BLK, None), P(GRP_BLK, None, None), P(), P(GRP_BLK), P(GRP_BLK, None)),
        out_specs=(P(GRP_BLK, None), P(GRP_BLK, None), P(GRP_BLK, None)),
        check_vma=False,
    )
```

time: 218 us -> 109 us (0.50)
  waiting for transfers between devices: 87.9 us -> 8.42 us
  local copies, waits for them, and re-layouts: 22 us -> 2.42 us
  Pallas kernels: 0 us -> 15.8 us
  matrix products: 15.2 us -> 0 us
  between operations: 14.3 us -> 0.66 us
  starting transfers between devices: 5.6 us -> 14.9 us
  other arithmetic: 7.78 us -> 2.82 us
    reduce_scatter x2 -> x0, waiting for transfers between devices: 84.2 us -> none  [reduced_to_own(): tiles = lax.psum_scatter(tiles, axes[k], scatter_dimension=0, tiled=True)]
    unnamed x1 -> x0, blocking collectives: 29.7 us -> none
    all_to_all x2 -> x4, blocking collectives: 34.7 us -> 63.3 us  [the longest x3 51 us: summed_over(): lax.all_to_all(pieces, axis, split_axis=0, concat_axis=0, tiled=True)]
    pallas_call x0 -> x3, Pallas kernels: none -> 15.8 us  [call(): pl.pallas_call(body, name=name, in_specs=[smem] * len(scalars) + [vmem] *...]
    dot_general x15 -> x0, matrix products: 15.2 us -> none  [the longest x3 5.45 us: layer_forward(): preact = jnp.dot(normed, weight, preferred_element_type=jnp.float32)]
    rev x2 -> x0, local copies, waits for them, and re-layouts: 9.02 us -> none  [flip_rows(): blocks.reshape(count, height // 2, 2, width)[:, :, ::-1, :]]
    all_to_all x1, starting transfers between devices: 5.56 us -> 12.9 us  [local(): lax.all_to_all(sent, 'grp', split_axis=0, concat_axis=0, tiled=True)]
    convert_element_type x2 -> x0, local copies, waits for them, and re-layouts: 2.98 us -> none  [the longest x1 1.98 us: local(): grad_second = grad_summed + grad_sent.astype(jnp.float32)]
  transfers between devices with their start and end apart: 3 -> 2, of which waited for: 3 -> 2; matrix products, arithmetic and copies ran while one was open for 2% -> 1% of each run, Pallas kernels for 0% -> 0%
where the time goes in v1:
time: 109 us; the launch traced here: 108 us
  blocking collectives  63.3 us (58%)
  Pallas kernels  15.8 us (14%)
  starting transfers between devices  14.9 us (14%)
  waiting for transfers between devices  8.42 us (8%)
  other arithmetic  2.82 us (3%)
  local copies, waits for them, and re-layouts  2.42 us (2%)
    all_to_all x3, blocking collectives, summed_over(): lax.all_to_all(pieces, axis, split_axis=0, concat_axis=0, tiled=True)  51 us
    pallas_call x3, Pallas kernels, call(): pl.pallas_call(body, name=name, in_specs=[smem] * len(scalars) + [vmem] *...  15.8 us
    all_to_all x1, starting transfers between devices, local(): lax.all_to_all(sent, 'grp', split_axis=0, concat_axis=0, tiled=True)  12.9 us
    all_to_all x1, blocking collectives, local(): lax.all_to_all(sent_back, 'grp', split_axis=0, concat_axis=0, tiled=True)  12.3 us
    all_to_all x1, waiting for transfers between devices, local(): lax.all_to_all(sent, 'grp', split_axis=0, concat_axis=0, tiled=True)  5.96 us
    ppermute x1, waiting for transfers between devices, local(): other = lax.ppermute(send, 'blk_2', [(0, 1), (1, 0)])  2.46 us
    unnamed x3, local copies, waits for them, and re-layouts  2.4 us
  transfers between devices with their start and end apart: 2, of which 2 were waited for; matrix products, arithmetic and copies ran while one was open for 1% of the time, Pallas kernels for 0%

profile of v1, /device:TPU:2, one launch (start us, length us, event | category | flops | bytes accessed | tf_op | source)
XLA Modules:
  0.0 108.3 jit_solution(3967760567672147211)
XLA Ops:
  0.6 1.6 %copy.10 = bf16[24,16,16]{2,1,0:T(8,128)(2,1)} copy(bf16[24,16,16]{0,2,1:T(8,128)(2,1)} %param.7) | data formatting | bytes 24576 | tf_op args[1]
  2.2 4.2 %forward.1 = (f32[384,512]{1,0:T(8,128)}, f32[384,512]{1,0:T(8,128)}, f32[384,512]{1,0:T(8,128)}, f32[384,512]{1,0:T(8,128)}, bf16[4,128,512]{2,1,0:T(8,128)(2,1)}) custom-call(s32[3]{0:T(128)} %partner_ref.5, bf16[384,512]{1,0:T(8,128)(2,1)} %edge_ref.1, bf16[384,16]{1,0:T(8,128)(2,1)} %bitcast.4, bf16[3,512,512]{2,1,0:T(8,128)(2,1)} %weight_ref.5), custom_call_target="tpu_custom_call" | custom-call | tf_op jit(solution)/shard_map/forward/pallas_call | solution.py:218
  6.4 12.9 %all-to-all-start = ((bf16[4,128,512]{2,1,0:T(8,128)(2,1)}), bf16[4,128,512]{2,1,0:T(8,128)(2,1)S(1)}, u32[]{:S(2)}, u32[]{:S(2)}) async-start(bf16[4,128,512]{2,1,0:T(8,128)(2,1)} %get-tuple-element.17), calls=%async_computation | async-start | bytes 1048576 | tf_op jit(solution)/shard_map/all_to_all | solution.py:246
  19.4 0.7 pad_add_fusion.index_ref
  20.0 6.0 %all-to-all-done.arrived_ref = bf16[4,128,512]{2,1,0:T(8,128)(2,1)S(1)} async-done(((bf16[4,128,512]{2,1,0:T(8,128)(2,1)}), bf16[4,128,512]{2,1,0:T(8,128)(2,1)S(1)}, u32[]{:S(2)}, u32[]{:S(2)}) %all-to-all-start) | async-done | bytes 524320 | tf_op jit(solution)/shard_map/all_to_all | solution.py:246
  26.0 0.0 copy-start
  26.0 0.8 copy-done
  26.8 4.4 %middle.1 = (bf16[384,512]{1,0:T(8,128)(2,1)}, f32[384,512]{1,0:T(8,128)}, bf16[384,512]{1,0:T(8,128)(2,1)}, bf16[384,512]{1,0:T(8,128)(2,1)}, bf16[4,128,512]{2,1,0:T(8,128)(2,1)}) custom-call(s32[3]{0:T(128)} %partner_ref.5, s32[2]{0:T(128)} %pad_add_fusion.index_ref, f32[384,512]{1,0:T(8,128)} %get-tuple-element.16.second_ref, ...), custom_call_target="tpu_custom_call" | custom-call | tf_op jit(solution)/shard_map/middle/pallas_call | solution.py:218
  31.2 12.3 %all_to_all.25.arrived_ref = bf16[4,128,512]{2,1,0:T(8,128)(2,1)} all-to-all(bf16[4,128,512]{2,1,0:T(8,128)(2,1)} %get-tuple-element.20), channel_id=1, replica_groups=mesh['grp'=4,'blk_0'=12,'blk_1'=8,'blk_2'=2] {'grp'}, dimensions={0} | all-to-all | bytes 1048576 | tf_op jit(solution)/shard_map/all_to_all | solution.py:251
  43.4 7.3 %backward.1 = (bf16[384,512]{1,0:T(8,128)(2,1)}, bf16[4,192,512]{2,1,0:T(8,128)(2,1)}, bf16[4,192,512]{2,1,0:T(8,128)(2,1)}) custom-call(s32[3]{0:T(128)} %partner_ref.5, s32[2]{0:T(128)} %pad_add_fusion.index_ref, f32[384,512]{1,0:T(8,128)} %get-tuple-element.19.grad_summed_ref, bf16[4,128,512]{2,1,0:T(8,128)(2,1)} %all_to_all.25.arrived_ref, ...), custom_call_target="tpu_custom_call" | custom-call | tf_op jit(solution)/shard_map/backward/pallas_call | solution.py:218
  50.7 1.9 %collective-permute-start = (bf16[4,192,512]{2,1,0:T(8,128)(2,1)}, bf16[4,192,512]{2,1,0:T(8,128)(2,1)S(1)}, u32[]{:S(2)}, u32[]{:S(2)}) collective-permute-start(bf16[4,192,512]{2,1,0:T(8,128)(2,1)} %get-tuple-element.28), channel_id=1, source_target_pairs={{0,1},{1,0},{2,3},{3,2},{4,5},{5,4},{6,7},{7,6},{8,9},{9,8},{10,11... | collective-permute-start | bytes 2359304 | tf_op jit(solution)/shard_map/ppermute | solution.py:262
  52.6 2.5 %collective-permute-done = bf16[4,192,512]{2,1,0:T(8,128)(2,1)S(1)} collective-permute-done((bf16[4,192,512]{2,1,0:T(8,128)(2,1)}, bf16[4,192,512]{2,1,0:T(8,128)(2,1)S(1)}, u32[]{:S(2)}, u32[]{:S(2)}) %collective-permute-start) | collective-permute-done | bytes 786464 | tf_op jit(solution)/shard_map/ppermute | solution.py:262
  55.1 1.3 %add_convert_fusion = bf16[4,192,512]{2,1,0:T(8,128)(2,1)S(1)} fusion(bf16[4,192,512]{2,1,0:T(8,128)(2,1)S(1)} %collective-permute-done, bf16[4,192,512]{2,1,0:T(8,128)(2,1)} %get-tuple-element.27), kind=kLoop, calls=%fused_computation | loop fusion | flops 1572864 | bytes 2359296 | tf_op jit(solution)/shard_map/convert_element_type | solution.py:263
  56.4 15.3 %all_to_all.26 = bf16[4,192,512]{2,1,0:T(8,128)(2,1)S(1)} all-to-all(bf16[4,192,512]{2,1,0:T(8,128)(2,1)S(1)} %add_convert_fusion), channel_id=1, replica_groups=mesh['grp'=4,'blk_0'=12,'blk_1'=8,'blk_2'=2] {'grp'}, dimensions={0} | all-to-all | bytes 1572864 | tf_op jit(solution)/shard_map/all_to_all | solution.py:229
  71.7 0.1 reduce_sum.33
  71.9 12.6 %all_to_all.27 = bf16[8,24,512]{2,1,0:T(8,128)(2,1)S(1)} all-to-all(bf16[8,24,512]{2,1,0:T(8,128)(2,1)S(1)} %bitcast.6), channel_id=1, replica_groups=mesh['grp'=4,'blk_0'=12,'blk_1'=8,'blk_2'=2] {'blk_1'}, dimensions={0} | all-to-all | bytes 393216 | tf_op jit(solution)/shard_map/all_to_all | solution.py:229
  84.5 23.1 %all_to_all.28 = bf16[12,2,512]{2,1,0:T(2,128)(2,1)S(1)} all-to-all(bf16[12,2,512]{2,1,0:T(2,128)(2,1)S(1)} %reshape.17), channel_id=1, replica_groups=mesh['grp'=4,'blk_0'=12,'blk_1'=8,'blk_2'=2] {'blk_0'}, dimensions={0} | all-to-all | bytes 49152 | tf_op jit(solution)/shard_map/all_to_all | solution.py:229
  107.7 0.6 broadcast_multiply_fusion
  (3 shorter events, 0.1 us)
Async XLA Ops:
  6.4 19.6 %all-to-all-start = ((bf16[4,128,512]{2,1,0:T(8,128)(2,1)}), bf16[4,128,512]{2,1,0:T(8,128)(2,1)S(1)}, u32[]{:S(2)}, u32[]{:S(2)}) async-start(bf16[4,128,512]{2,1,0:T(8,128)(2,1)} %get-tuple-element.17), calls=%async_computation | async-start | bytes 1048576 | tf_op jit(solution)/shard_map/all_to_all | solution.py:246
  26.0 0.8 copy-start
  50.7 4.4 %collective-permute-start = (bf16[4,192,512]{2,1,0:T(8,128)(2,1)}, bf16[4,192,512]{2,1,0:T(8,128)(2,1)S(1)}, u32[]{:S(2)}, u32[]{:S(2)}) collective-permute-start(bf16[4,192,512]{2,1,0:T(8,128)(2,1)} %get-tuple-element.28), channel_id=1, source_target_pairs={{0,1},{1,0},{2,3},{3,2},{4,5},{5,4},{6,7},{7,6},{8,9},{9,8},{10,11... | collective-permute-start | bytes 2359304 | tf_op jit(solution)/shard_map/ppermute | solution.py:262

commit v2 on v1

--- a/solution.py
+++ b/solution.py
@@ -45,7 +45,8 @@
     return upstream + inverse * (grad_normed - unit * inner), grad_pre
 
 
-def basis_blocks(basis, count):
+def basis_blocks(basis_ref, count):
+    basis = basis_ref[...].reshape(count * BLOCK, NBR)
     wide_row = lax.broadcasted_iota(jnp.int32, (NBR, BLOCK), 0)
     wide_col = lax.broadcasted_iota(jnp.int32, (NBR, BLOCK), 1)
     spread = jnp.where(wide_col % NBR == wide_row, 1.0, 0.0).astype(BF16)
@@ -89,10 +90,10 @@
     return jnp.concatenate(picked, axis=0)
 
 
-def forward_body(partner_ref, edge_ref, basis_ref, weight_ref, mixed_ref, pre_one_ref, pre_two_ref,
+def forward_body(partner_ref, index_ref, edge_ref, basis_ref, weight_ref, mixed_ref, pre_one_ref, pre_two_ref,
                  second_ref, slots_ref, sent_ref):
     count = edge_ref.shape[0] // BLOCK
-    blocks = basis_blocks(basis_ref[...], count)
+    blocks = basis_blocks(basis_ref, count)
     mixed = jnp.concatenate(
         [dot(blocks[n], edge_ref[n * BLOCK : (n + 1) * BLOCK, :]) for n in range(count)], axis=0
     )
@@ -195,7 +196,7 @@
         unit_one, inverse_one, pre_one, weight_ref[0], grad_first
     )
     grad_round = grad_mixed.astype(BF16)
-    blocks = basis_blocks(basis_ref[...], count)
+    blocks = basis_blocks(basis_ref, count)
     for n in range(count):
         rows = slice(n * BLOCK, (n + 1) * BLOCK)
         grad_state_ref[rows, :] = dot_tn(blocks[n], grad_round[rows]).astype(BF16)
@@ -212,6 +213,10 @@
     send_ref[...] = wide_ref[1].astype(BF16)
 
 
+def near(array):
+    return pltpu.with_memory_space_constraint(array, pltpu.VMEM)
+
+
 def call(body, name, scalars, arrays, outs, scratch):
     smem = pl.BlockSpec(memory_space=pltpu.SMEM)
     vmem = pl.BlockSpec(memory_space=pltpu.VMEM)
@@ -220,9 +225,10 @@
         name=name,
         in_specs=[smem] * len(scalars) + [vmem] * len(arrays),
         out_specs=[vmem] * len(outs),
-        out_shape=[jax.ShapeDtypeStruct(*o) for o in outs],
+        out_shape=[pltpu.VMEM(*o) for o in outs],
         scratch_shapes=[pltpu.VMEM(*s) for s in scratch],
-    )(*scalars, *arrays)
+        compiler_params=pltpu.CompilerParams(vmem_limit_bytes=24 * 1024 * 1024),
+    )(*scalars, *[near(array) for array in arrays])
 
 
 def summed_over(pieces, axis):
@@ -235,12 +241,11 @@
     groups, deep, high, cores = (lax.axis_size(a) for a in GRP_BLK)
     total_edges = rows * groups * deep * high * cores
     index = jnp.stack([lax.axis_index("grp"), lax.axis_index("blk_2")]).astype(jnp.int32)
-    flat_basis = basis.reshape(rows, NBR)
     full = ((rows, width), F32)
     half = ((rows, width), BF16)
     slots = ((groups, BLOCK, width), BF16)
     mixed, pre_one, pre_two, second, sent = call(
-        forward_body, "forward", [partner], [edge_state, flat_basis, weights],
+        forward_body, "forward", [partner, index], [edge_state, basis, weights],
         [full, full, full, full, slots], [half],
     )
     arrived = lax.all_to_all(sent, "grp", split_axis=0, concat_axis=0, tiled=True)
@@ -255,7 +260,7 @@
     grad_state, keep, send = call(
         functools.partial(backward_body, high=high), "backward", [partner, index],
         [grad_summed, returned, mixed, pre_one, pre_two, normed_three, grad_pre_three, weights,
-         flat_basis, order],
+         basis, order],
         [half, (pieces, BF16), (pieces, BF16)],
         [((2, *pieces), F32)],
     )

time: 109 us -> 100 us (0.917)
  Pallas kernels: 15.8 us -> 7.85 us
  blocking collectives: 63.3 us -> 57.2 us
  local copies, waits for them, and re-layouts: 2.42 us -> 6.15 us
  waiting for transfers between devices: 8.42 us -> 11.2 us
  other arithmetic: 2.82 us -> 1.1 us
    all_to_all x3 -> x2, blocking collectives: 51 us -> 27.9 us  [summed_over(): lax.all_to_all(pieces, axis, split_axis=0, concat_axis=0, tiled=True)]
    all_to_all x0 -> x1, blocking collectives: none -> 18.8 us  [local(): lax.all_to_all(sent, 'grp', split_axis=0, concat_axis=0, tiled=True)]
    pallas_call x3, Pallas kernels: 15.8 us -> 7.85 us  [call(): pl.pallas_call(body, name=name, in_specs=[smem] * len(scalars) + [vmem] *...]
    unnamed x3 -> x15, local copies, waits for them, and re-layouts: 2.4 us -> 5.54 us
    all_to_all x1, waiting for transfers between devices: 5.96 us -> 8.95 us  [summed_over(): lax.all_to_all(pieces, axis, split_axis=0, concat_axis=0, tiled=True)]
    all_to_all x1, blocking collectives: 12.3 us -> 10.5 us  [local(): lax.all_to_all(sent_back, 'grp', split_axis=0, concat_axis=0, tiled=True)]
    convert_element_type x1, other arithmetic: 1.34 us -> 0.21 us  [local(): pair = (keep.astype(F32) + other.astype(F32)).astype(BF16)]
where the time goes in v2:
time: 100 us; the launch traced here: 99.8 us
  blocking collectives  57.2 us (57%)
  starting transfers between devices  15.7 us (16%)
  waiting for transfers between devices  11.2 us (11%)
  Pallas kernels  7.85 us (8%)
  local copies, waits for them, and re-layouts  6.15 us (6%)
  other arithmetic  1.1 us (1%)
    all_to_all x2, blocking collectives, summed_over(): lax.all_to_all(pieces, axis, split_axis=0, concat_axis=0, tiled=True)  27.9 us
    all_to_all x1, blocking collectives, local(): lax.all_to_all(sent, 'grp', split_axis=0, concat_axis=0, tiled=True)  18.8 us
    all_to_all x1, starting transfers between devices, summed_over(): lax.all_to_all(pieces, axis, split_axis=0, concat_axis=0, tiled=True)  13.7 us
    all_to_all x1, blocking collectives, local(): lax.all_to_all(sent_back, 'grp', split_axis=0, concat_axis=0, tiled=True)  10.5 us
    all_to_all x1, waiting for transfers between devices, summed_over(): lax.all_to_all(pieces, axis, split_axis=0, concat_axis=0, tiled=True)  8.95 us
    pallas_call x3, Pallas kernels, call(): pl.pallas_call(body, name=name, in_specs=[smem] * len(scalars) + [vmem] *...  7.85 us
    unnamed x15, local copies, waits for them, and re-layouts  5.54 us
    ppermute x1, waiting for transfers between devices, local(): other = lax.ppermute(send, 'blk_2', [(0, 1), (1, 0)])  2.25 us
  transfers between devices with their start and end apart: 2, of which 2 were waited for; matrix products, arithmetic and copies ran while one was open for 1% of the time, Pallas kernels for 0%

profile of v2, /device:TPU:2, one launch (start us, length us, event | category | flops | bytes accessed | tf_op | source)
XLA Modules:
  0.0 99.8 jit_solution(6472047308118956256)
XLA Ops:
  0.6 1.0 copy.11.basis_ref
  1.6 0.1 pad_add_fusion.index_ref
  1.7 1.4 %copy-done = bf16[3,512,512]{2,1,0:T(8,128)(2,1)S(1)} copy-done((bf16[3,512,512]{2,1,0:T(8,128)(2,1)S(1)}, bf16[3,512,512]{2,1,0:T(8,128)(2,1)}, u32[]{:S(2)}) %copy-start) | copy-done | bytes 1572888
  3.1 1.0 copy-done.2
  4.1 0.7 copy-done.5
  4.8 1.9 %forward.1 = (f32[384,512]{1,0:T(8,128)S(1)}, f32[384,512]{1,0:T(8,128)S(1)}, f32[384,512]{1,0:T(8,128)S(1)}, f32[384,512]{1,0:T(8,128)S(1)}, bf16[4,128,512]{2,1,0:T(8,128)(2,1)S(1)}) custom-call(s32[3]{0:T(128)S(1)} %copy-done.5, s32[2]{0:T(128)S(1)} %pad_add_fusion.index_ref, bf16[384,512]{1,0:T(8,128)(2,1)S(1)} %copy-done.2, ...), custom_call_target="tpu_custom_call" | custom-call | tf_op jit(solution)/shard_map/forward/pallas_call | solution.py:223
  6.7 18.8 %all_to_all.25.arrived_ref = bf16[4,128,512]{2,1,0:T(8,128)(2,1)S(1)} all-to-all(bf16[4,128,512]{2,1,0:T(8,128)(2,1)S(1)} %get-tuple-element.17), channel_id=1, replica_groups=mesh['grp'=4,'blk_0'=12,'blk_1'=8,'blk_2'=2] {'grp'}, dimensions={0} | all-to-all | bytes 1048576 | tf_op jit(solution)/shard_map/all_to_all | solution.py:251
  25.5 0.0 copy-done.1
  25.5 0.0 copy-done.3
  25.5 1.9 %middle.1 = (bf16[384,512]{1,0:T(8,128)(2,1)S(1)}, f32[384,512]{1,0:T(8,128)S(1)}, bf16[384,512]{1,0:T(8,128)(2,1)S(1)}, bf16[384,512]{1,0:T(8,128)(2,1)S(1)}, bf16[4,128,512]{2,1,0:T(8,128)(2,1)S(1)}) custom-call(s32[3]{0:T(128)S(1)} %copy-done.5, s32[2]{0:T(128)S(1)} %pad_add_fusion.index_ref, f32[384,512]{1,0:T(8,128)S(1)} %get-tuple-element.16.second_ref, ...), custom_call_target="tpu_custom_call" | custom-call | tf_op jit(solution)/shard_map/middle/pallas_call | solution.py:223
  27.4 10.5 %all_to_all.26.arrived_ref = bf16[4,128,512]{2,1,0:T(8,128)(2,1)S(1)} all-to-all(bf16[4,128,512]{2,1,0:T(8,128)(2,1)S(1)} %get-tuple-element.20), channel_id=1, replica_groups=mesh['grp'=4,'blk_0'=12,'blk_1'=8,'blk_2'=2] {'grp'}, dimensions={0} | all-to-all | bytes 1048576 | tf_op jit(solution)/shard_map/all_to_all | solution.py:256
  37.9 4.1 %backward.1 = (bf16[384,512]{1,0:T(8,128)(2,1)S(1)}, bf16[4,192,512]{2,1,0:T(8,128)(2,1)S(1)}, bf16[4,192,512]{2,1,0:T(8,128)(2,1)S(1)}) custom-call(s32[3]{0:T(128)S(1)} %copy-done.5, s32[2]{0:T(128)S(1)} %pad_add_fusion.index_ref, f32[384,512]{1,0:T(8,128)S(1)} %get-tuple-element.19.grad_summed_ref, bf16[4,128,512]{2,1,0:T(8,128)(2,1)S(1)} %all_to_all.26.arrived_ref, ...), custom_call_target="tpu_custom_call" | custom-call | tf_op jit(solution)/shard_map/backward/pallas_call | solution.py:223
  42.0 1.9 %collective-permute-start = (bf16[4,192,512]{2,1,0:T(8,128)(2,1)S(1)}, bf16[4,192,512]{2,1,0:T(8,128)(2,1)S(1)}, u32[]{:S(2)}, u32[]{:S(2)}) collective-permute-start(bf16[4,192,512]{2,1,0:T(8,128)(2,1)S(1)} %get-tuple-element.28), channel_id=1, source_target_pairs={{0,1},{1,0},{2,3},{3,2},{4,5},{5,4},{6,7},{7,6},{8,9},{9,8},{10,11... | collective-permute-start | bytes 2359304 | tf_op jit(solution)/shard_map/ppermute | solution.py:267
  43.9 2.3 %collective-permute-done = bf16[4,192,512]{2,1,0:T(8,128)(2,1)S(1)} collective-permute-done((bf16[4,192,512]{2,1,0:T(8,128)(2,1)S(1)}, bf16[4,192,512]{2,1,0:T(8,128)(2,1)S(1)}, u32[]{:S(2)}, u32[]{:S(2)}) %collective-permute-start) | collective-permute-done | bytes 786464 | tf_op jit(solution)/shard_map/ppermute | solution.py:267
  46.1 0.2 add_convert_fusion
  46.4 15.3 %all_to_all.27 = bf16[4,192,512]{2,1,0:T(8,128)(2,1)S(1)} all-to-all(bf16[4,192,512]{2,1,0:T(8,128)(2,1)S(1)} %add_convert_fusion), channel_id=1, replica_groups=mesh['grp'=4,'blk_0'=12,'blk_1'=8,'blk_2'=2] {'grp'}, dimensions={0} | all-to-all | bytes 1572864 | tf_op jit(solution)/shard_map/all_to_all | solution.py:235
  61.6 0.1 reduce_sum.33
  61.8 12.6 %all_to_all.28 = bf16[8,24,512]{2,1,0:T(8,128)(2,1)S(1)} all-to-all(bf16[8,24,512]{2,1,0:T(8,128)(2,1)S(1)} %bitcast.3), channel_id=1, replica_groups=mesh['grp'=4,'blk_0'=12,'blk_1'=8,'blk_2'=2] {'blk_1'}, dimensions={0} | all-to-all | bytes 393216 | tf_op jit(solution)/shard_map/all_to_all | solution.py:235
  74.4 0.6 reshape.13
  75.0 13.7 %all-to-all-start.4 = ((bf16[12,2,512]{2,1,0:T(2,128)(2,1)}), bf16[12,2,512]{2,1,0:T(2,128)(2,1)S(1)}, u32[]{:S(2)}, u32[]{:S(2)}) async-start(bf16[12,2,512]{2,1,0:T(2,128)(2,1)} %reshape.13), calls=%async_computation.4 | async-start | bytes 49152 | tf_op jit(solution)/shard_map/all_to_all | solution.py:235
  88.8 0.7 copy.13
  89.5 0.7 copy.14
  90.3 8.9 %all-to-all-done.4 = bf16[12,2,512]{2,1,0:T(2,128)(2,1)S(1)} async-done(((bf16[12,2,512]{2,1,0:T(2,128)(2,1)}), bf16[12,2,512]{2,1,0:T(2,128)(2,1)S(1)}, u32[]{:S(2)}, u32[]{:S(2)}) %all-to-all-start.4) | async-done | bytes 24608 | tf_op jit(solution)/shard_map/all_to_all | solution.py:235
  99.2 0.6 broadcast_multiply_fusion
  (9 shorter events, 0.1 us)
Async XLA Ops:
  1.7 1.4 %copy-start = (bf16[3,512,512]{2,1,0:T(8,128)(2,1)S(1)}, bf16[3,512,512]{2,1,0:T(8,128)(2,1)}, u32[]{:S(2)}) copy-start(bf16[3,512,512]{2,1,0:T(8,128)(2,1)} %weight_ref.5) | copy-start | bytes 4718596
  3.1 1.0 copy-start.2
  4.1 0.7 copy-start.5
  4.8 20.8 %copy-start.1 = (bf16[3,512,512]{2,1,0:T(8,128)(2,1)S(1)}, bf16[3,512,512]{2,1,0:T(8,128)(2,1)}, u32[]{:S(2)}) copy-start(bf16[3,512,512]{2,1,0:T(8,128)(2,1)} %weight_ref.5) | copy-start | bytes 4718596
  4.8 20.8 %copy-start.3 = (bf16[384,512]{1,0:T(8,128)(2,1)S(1)}, bf16[384,512]{1,0:T(8,128)(2,1)}, u32[]{:S(2)}) copy-start(bf16[384,512]{1,0:T(8,128)(2,1)} %cotangent_ref.1) | copy-start | bytes 1179652
  25.5 12.4 %copy-start.4 = (s32[3,512]{1,0:T(4,128)S(1)}, s32[3,512]{1,0:T(4,128)}, u32[]{:S(2)}) copy-start(s32[3,512]{1,0:T(4,128)} %constant.18.clone.order_ref) | copy-start | bytes 18436
  42.0 4.2 %collective-permute-start = (bf16[4,192,512]{2,1,0:T(8,128)(2,1)S(1)}, bf16[4,192,512]{2,1,0:T(8,128)(2,1)S(1)}, u32[]{:S(2)}, u32[]{:S(2)}) collective-permute-start(bf16[4,192,512]{2,1,0:T(8,128)(2,1)S(1)} %get-tuple-element.28), channel_id=1, source_target_pairs={{0,1},{1,0},{2,3},{3,2},{4,5},{5,4},{6,7},{7,6},{8,9},{9,8},{10,11... | collective-permute-start | bytes 2359304 | tf_op jit(solution)/shard_map/ppermute | solution.py:267
  75.0 24.2 %all-to-all-start.4 = ((bf16[12,2,512]{2,1,0:T(2,128)(2,1)}), bf16[12,2,512]{2,1,0:T(2,128)(2,1)S(1)}, u32[]{:S(2)}, u32[]{:S(2)}) async-start(bf16[12,2,512]{2,1,0:T(2,128)(2,1)} %reshape.13), calls=%async_computation.4 | async-start | bytes 49152 | tf_op jit(solution)/shard_map/all_to_all | solution.py:235

commit v3 on v2

v3 whole, which is shorter than its diff:
```python
import functools
import math

import jax
import jax.numpy as jnp
import numpy as np
from jax import lax
from jax.experimental import pallas as pl
from jax.experimental.pallas import tpu as pltpu
from jax.sharding import Mesh
from jax.sharding import PartitionSpec as P

NBR = 16
BLOCK = 128
GRP_BLK = ("grp", "blk_0", "blk_1", "blk_2")
BF16 = jnp.bfloat16
F32 = jnp.float32


def dot(a, b):
    return jnp.dot(a, b, preferred_element_type=F32)


def dot_nt(a, b):
    return lax.dot_general(a, b, (((1,), (1,)), ((), ())), preferred_element_type=F32)


def dot_tn(a, b):
    return lax.dot_general(a, b, (((0,), (0,)), ((), ())), preferred_element_type=F32)


def inverse_norm(hidden):
    return lax.rsqrt(jnp.mean(hidden * hidden, axis=-1, keepdims=True) + 1e-06)


def sigmoid(v):
    return 0.5 + 0.5 * jnp.tanh(0.5 * v)


def layer_backward(unit, inverse, preact, weight, upstream):
    sigma = sigmoid(preact)
    grad_pre = (upstream * sigma * (1.0 + preact * (1.0 - sigma))).astype(BF16)
    grad_normed = dot_nt(grad_pre, weight)
    inner = jnp.mean(grad_normed * unit, axis=-1, keepdims=True)
    return upstream + inverse * (grad_normed - unit * inner), grad_pre


def basis_blocks(turned, atoms):
    pairs = NBR * NBR
    rows = atoms * NBR
    row = lax.broadcasted_iota(jnp.int32, (rows, atoms), 0)
    col = lax.broadcasted_iota(jnp.int32, (rows, atoms), 1)
    repeat = jnp.where(row // NBR == col, 1.0, 0.0).astype(BF16)
    wide = dot_nt(repeat, turned)
    row = lax.broadcasted_iota(jnp.int32, (rows, pairs), 0)
    col = lax.broadcasted_iota(jnp.int32, (rows, pairs), 1)
    wide = jnp.where(row % NBR == col // NBR, wide, 0.0).astype(BF16)
    row = lax.broadcasted_iota(jnp.int32, (pairs, BLOCK), 0)
    col = lax.broadcasted_iota(jnp.int32, (pairs, BLOCK), 1)
    tiled = dot(wide, jnp.where(row % NBR == col % NBR, 1.0, 0.0).astype(BF16))
    row = lax.broadcasted_iota(jnp.int32, (rows, BLOCK), 0)
    col = lax.broadcasted_iota(jnp.int32, (rows, BLOCK), 1)
    return jnp.where((row % BLOCK) // NBR == col // NBR, tiled, 0.0).astype(BF16)


def owner_of(number, count):
    owner = jnp.int32(0)
    for edge in range(1, 4):
        owner = owner + (number >= edge * count).astype(jnp.int32)
    return owner


def fill_slots(slots_ref, blocks_ref, scalar_ref, group_count, count):
    owners = [owner_of(scalar_ref[n], count) for n in range(count)]
    for d in range(group_count):
        pick = jnp.int32(0)
        for n in range(1, count):
            pick = jnp.where(owners[n] == d, n, pick)
        start = pl.multiple_of(pick * BLOCK, BLOCK)
        slots_ref[d] = blocks_ref[pl.ds(start, BLOCK), :]


def reverse_blocks(arrived_ref, own_ref, scalar_ref, count):
    row = lax.broadcasted_iota(jnp.int32, (BLOCK, BLOCK), 0)
    col = lax.broadcasted_iota(jnp.int32, (BLOCK, BLOCK), 1)
    flip = jnp.where(row + 1 - 2 * (row % 2) == col, 1.0, 0.0).astype(BF16)
    picked = []
    for n in range(count):
        number = scalar_ref[n]
        owner = owner_of(number, count)
        start = pl.multiple_of((number - owner * count) * BLOCK, BLOCK)
        near = own_ref[pl.ds(start, BLOCK), :].astype(BF16)
        picked.append(dot(flip, jnp.where(owner == scalar_ref[count], near, arrived_ref[owner])))
    return jnp.concatenate(picked, axis=0)


def forward_body(scalar_ref, edge_hbm, turned_hbm, weight_hbm, mixed_ref, pre_one_ref, pre_two_ref,
                 second_ref, slots_ref, blocks_ref, weight_ref, edge_ref, turned_ref, sent_ref, sems):
    rows = edge_ref.shape[0]
    count = rows // BLOCK
    turned_copy = pltpu.make_async_copy(turned_hbm, turned_ref, sems.at[0])
    edge_copy = pltpu.make_async_copy(edge_hbm, edge_ref, sems.at[1])
    weight_copies = [
        pltpu.make_async_copy(weight_hbm.at[n], weight_ref.at[n], sems.at[2 + n]) for n in range(3)
    ]
    turned_copy.start()
    edge_copy.start()
    for copy in weight_copies:
        copy.start()
    turned_copy.wait()
    blocks_ref[...] = basis_blocks(turned_ref[...], rows // NBR)
    edge_copy.wait()
    mixed = jnp.concatenate(
        [
            dot(blocks_ref[n * BLOCK : (n + 1) * BLOCK, :], edge_ref[n * BLOCK : (n + 1) * BLOCK, :])
            for n in range(count)
        ],
        axis=0,
    )
    mixed_ref[...] = mixed
    normed = (mixed * inverse_norm(mixed)).astype(BF16)
    weight_copies[0].wait()
    pre_one = dot(normed, weight_ref[0])
    pre_one_ref[...] = pre_one
    first = mixed + pre_one * sigmoid(pre_one)
    normed = (first * inverse_norm(first)).astype(BF16)
    weight_copies[1].wait()
    pre_two = dot(normed, weight_ref[1])
    pre_two_ref[...] = pre_two
    second = first + pre_two * sigmoid(pre_two)
    second_ref[...] = second
    sent_ref[...] = second.astype(BF16)
    fill_slots(slots_ref, sent_ref, scalar_ref, slots_ref.shape[0], count)
    weight_copies[2].wait()


def middle_body(scalar_ref, second_ref, arrived_ref, weight_ref, cotangent_ref, edge_out_hbm,
                grad_summed_ref, normed_ref, grad_pre_ref, slots_ref, sent_ref, edge_out_ref, sems):
    count = second_ref.shape[0] // BLOCK
    summed = second_ref[...] + reverse_blocks(arrived_ref, second_ref, scalar_ref, count)
    inverse = inverse_norm(summed)
    unit = summed * inverse
    normed = unit.astype(BF16)
    normed_ref[...] = normed
    preact = dot(normed, weight_ref[2])
    edge_out_ref[...] = (summed + preact * sigmoid(preact)).astype(BF16)
    copy = pltpu.make_async_copy(edge_out_ref, edge_out_hbm, sems.at[0])
    copy.start()
    grad_summed, grad_pre = layer_backward(
        unit, inverse, preact, weight_ref[2], cotangent_ref[...].astype(F32)
    )
    grad_pre_ref[...] = grad_pre
    grad_summed_ref[...] = grad_summed
    sent_ref[...] = grad_summed.astype(BF16)
    fill_slots(slots_ref, sent_ref, scalar_ref, slots_ref.shape[0], count)
    copy.wait()


def layer_pieces(layer, groups, deep):
    per_layer = groups * deep // 3
    pieces = []
    done = 0
    while done < per_layer:
        number = per_layer * layer + done
        size = min(per_layer - done, deep - number % deep)
        pieces.append((number // deep, number % deep, done, size))
        done += size
    return pieces


def row_order(groups, deep, high, cores):
    order = []
    for layer in range(3):
        rows = []
        for _, _, done, size in layer_pieces(layer, groups, deep):
            y, z, i = np.meshgrid(np.arange(high), np.arange(size), np.arange(2), indexing="ij")
            rows.append((2 * cores * high * (z + done) + 2 * cores * y + i).reshape(-1))
        rows = np.concatenate(rows)
        order.append(np.concatenate([rows, rows]))
    return np.stack(order).astype(np.int32)


def permuted(normed, order, core):
    width = normed.shape[1]
    place = lax.broadcasted_iota(jnp.int32, (1, width), 1)
    source = order + 2 * jnp.where(place < width // 2, core, 1 - core)
    row = lax.broadcasted_iota(jnp.int32, (width, width), 0)
    choice = jnp.where(row == source, 1.0, 0.0).astype(BF16)
    return dot(normed, choice).astype(BF16)


def halves(grad_weight, keep_ref, send_ref):
    half = grad_weight.shape[0] // 2
    keep_ref[...] = grad_weight[:half].astype(BF16)
    send_ref[...] = grad_weight[half:].astype(BF16)


def backward_body(scalar_ref, grad_summed_ref, arrived_ref, mixed_ref, pre_one_ref, pre_two_ref,
                  weight_ref, blocks_ref, order_ref, normed_three_ref,
                  grad_pre_three_ref, grad_state_hbm, keep_ref, send_ref, grad_state_ref, sems):
    count = mixed_ref.shape[0] // BLOCK
    core = scalar_ref[count + 1]
    mixed = mixed_ref[...]
    pre_one = pre_one_ref[...]
    pre_two = pre_two_ref[...]
    grad_second = grad_summed_ref[...] + reverse_blocks(
        arrived_ref, grad_summed_ref, scalar_ref, count
    )
    first = mixed + pre_one * sigmoid(pre_one)
    inverse_two = inverse_norm(first)
    unit_two = first * inverse_two
    grad_first, grad_pre_two = layer_backward(
        unit_two, inverse_two, pre_two, weight_ref[1], grad_second
    )
    inverse_one = inverse_norm(mixed)
    unit_one = mixed * inverse_one
    grad_mixed, grad_pre_one = layer_backward(
        unit_one, inverse_one, pre_one, weight_ref[0], grad_first
    )
    grad_round = grad_mixed.astype(BF16)
    for n in range(count):
        rows = slice(n * BLOCK, (n + 1) * BLOCK)
        grad_state_ref[rows, :] = dot_tn(blocks_ref[rows, :], grad_round[rows]).astype(BF16)
    copy = pltpu.make_async_copy(grad_state_ref, grad_state_hbm, sems.at[0])
    copy.start()
    pairs = (
        (unit_one.astype(BF16), grad_pre_one),
        (unit_two.astype(BF16), grad_pre_two),
        (normed_three_ref[...], grad_pre_three_ref[...]),
    )
    for layer, (normed, grad_pre) in enumerate(pairs):
        ordered = permuted(normed, order_ref[layer : layer + 1, :], core)
        halves(dot_tn(ordered, grad_pre), keep_ref.at[layer], send_ref.at[layer])
    copy.wait()


def join_body(keep_ref, other_ref, pair_ref, wide_ref, *, high):
    groups, part = wide_ref.shape[:2]
    deep = part // (2 * high)
    for layer in range(3):
        rows = keep_ref[layer].astype(F32) + other_ref[layer].astype(F32)
        start = 0
        for g, z, _, size in layer_pieces(layer, groups, deep):
            for y in range(high):
                to = 2 * deep * y + 2 * z
                wide_ref[g, to : to + 2 * size, :] = rows[start : start + 2 * size]
                start += 2 * size
    pair_ref[...] = wide_ref[...].astype(BF16)


def plane_body(column_ref, plane_ref):
    total = column_ref[0].astype(F32)
    for y in range(1, column_ref.shape[0]):
        total = total + column_ref[y].astype(F32)
    deep, pair = plane_ref.shape[:2]
    for z in range(deep):
        plane_ref[z] = total[pair * z : pair * (z + 1)].astype(BF16)


def near(array):
    return pltpu.with_memory_space_constraint(array, pltpu.VMEM)


def away(array):
    return pltpu.with_memory_space_constraint(array, pltpu.HBM)


def call(body, name, scalars, far, arrays, far_outs, outs, scratch):
    smem = pl.BlockSpec(memory_space=pltpu.SMEM)
    vmem = pl.BlockSpec(memory_space=pltpu.VMEM)
    anywhere = pl.BlockSpec(memory_space=pltpu.HBM)
    return pl.pallas_call(
        body,
        name=name,
        in_specs=[smem] * len(scalars) + [anywhere] * len(far) + [vmem] * len(arrays),
        out_specs=[anywhere] * len(far_outs) + [vmem] * len(outs),
        out_shape=[jax.ShapeDtypeStruct(*o) for o in far_outs] + [pltpu.VMEM(*o) for o in outs],
        scratch_shapes=scratch,
        compiler_params=pltpu.CompilerParams(vmem_limit_bytes=24 * 1024 * 1024),
    )(*scalars, *[away(array) for array in far], *[near(array) for array in arrays])


def summed_over(pieces, axis):
    arrived = lax.all_to_all(pieces, axis, split_axis=0, concat_axis=0, tiled=True)
    return arrived.astype(F32).sum(axis=0)


def local(edge_state, basis, weights, partner, cotangent):
    rows, width = edge_state.shape
    groups, deep, high, cores = (lax.axis_size(a) for a in GRP_BLK)
    total_edges = rows * groups * deep * high * cores
    scalars = jnp.concatenate(
        [partner, jnp.stack([lax.axis_index("grp"), lax.axis_index("blk_2")]).astype(jnp.int32)]
    )
    turned = basis.transpose(1, 2, 0).reshape(NBR * NBR, rows // NBR)
    full = ((rows, width), F32)
    half = ((rows, width), BF16)
    slots = ((groups, BLOCK, width), BF16)
    mixed, pre_one, pre_two, second, sent, blocks, weights_near = call(
        forward_body, "forward", [scalars], [edge_state, turned, weights], [], [],
        [full, full, full, full, slots, ((rows, BLOCK), BF16), (weights.shape, BF16)],
        [pltpu.VMEM(*half), pltpu.VMEM(turned.shape, BF16), pltpu.VMEM(*half),
         pltpu.SemaphoreType.DMA((5,))],
    )
    arrived = lax.all_to_all(sent, "grp", split_axis=0, concat_axis=0, tiled=True)
    edge_out, grad_summed, normed_three, grad_pre_three, sent_back = call(
        middle_body, "middle", [scalars], [], [second, arrived, weights_near, cotangent],
        [half], [full, half, half, slots],
        [pltpu.VMEM(*half), pltpu.VMEM(*half), pltpu.SemaphoreType.DMA((1,))],
    )
    returned = lax.all_to_all(sent_back, "grp", split_axis=0, concat_axis=0, tiled=True)
    order = jnp.asarray(row_order(groups, deep, high, cores))
    swap = [(0, 1), (1, 0)]
    side = (width // 2, width)
    grad_state, keep, send = call(
        backward_body, "backward", [scalars], [],
        [grad_summed, returned, mixed, pre_one, pre_two, weights_near, blocks, order,
         normed_three, grad_pre_three],
        [half], [((3, *side), BF16), ((3, *side), BF16)],
        [pltpu.VMEM(*half), pltpu.SemaphoreType.DMA((1,))],
    )
    other = lax.ppermute(send, "blk_2", swap)
    part = 3 * width // (groups * cores)
    (pair,) = call(
        functools.partial(join_body, high=high), "join", [], [],
        [keep, other], [], [((groups, part, width), BF16)],
        [pltpu.VMEM((groups, part, width), F32)],
    )
    line = summed_over(pair, "grp").astype(BF16)
    column = lax.all_to_all(
        line.reshape(high, part // high, width), "blk_1", split_axis=0, concat_axis=0, tiled=True
    )
    (plane,) = call(
        plane_body, "plane", [], [], [column], [],
        [((deep, part // high // deep, width), BF16)], [],
    )
    final = summed_over(plane, "blk_0")
    return edge_out, grad_state, final * (1.0 / math.sqrt(total_edges))


def solution(mesh):
    split = Mesh(mesh.devices.reshape(mesh.shape["grp"], 12, 8, 2), GRP_BLK)
    return jax.shard_map(
        local,
        mesh=split,
        in_specs=(P(GRP_BLK, None), P(GRP_BLK, None, None), P(), P(GRP_BLK), P(GRP_BLK, None)),
        out_specs=(P(GRP_BLK, None), P(GRP_BLK, None), P(GRP_BLK, None)),
        check_vma=False,
    )
```

time: 100 us -> 97.7 us (0.977)
  blocking collectives: 57.2 us -> 81.1 us
  starting transfers between devices: 15.7 us -> 1.92 us
  waiting for transfers between devices: 11.2 us -> 2.25 us
  local copies, waits for them, and re-layouts: 6.15 us -> 0.01 us
  Pallas kernels: 7.85 us -> 9.76 us
    all_to_all x1 -> x0, starting transfers between devices: 13.7 us -> none  [summed_over(): lax.all_to_all(pieces, axis, split_axis=0, concat_axis=0, tiled=True)]
    all_to_all x0 -> x1, blocking collectives: none -> 12.6 us  [local(): lax.all_to_all(line.reshape(high, part // high, width), 'blk_1', split_ax...]
    all_to_all x2, blocking collectives: 27.9 us -> 39.5 us  [summed_over(): lax.all_to_all(pieces, axis, split_axis=0, concat_axis=0, tiled=True)]
    all_to_all x1 -> x0, waiting for transfers between devices: 8.95 us -> none  [summed_over(): lax.all_to_all(pieces, axis, split_axis=0, concat_axis=0, tiled=True)]
    unnamed x15 -> x4, local copies, waits for them, and re-layouts: 5.54 us -> 0.01 us
    pallas_call x3 -> x5, Pallas kernels: 7.85 us -> 9.76 us  [call(): pl.pallas_call(body, name=name, in_specs=[smem] * len(scalars) + [anywher...]
  transfers between devices with their start and end apart: 2 -> 1, of which waited for: 2 -> 1; matrix products, arithmetic and copies ran while one was open for 1% -> 0% of each run, Pallas kernels for 0% -> 0%
where the time goes in v3:
time: 97.7 us; the launch traced here: 97.3 us
  blocking collectives  81.1 us (83%)
  Pallas kernels  9.76 us (10%)
  waiting for transfers between devices  2.25 us (2%)
  starting transfers between devices  1.92 us (2%)
  other arithmetic  1.56 us (2%)
    all_to_all x2, blocking collectives, summed_over(): lax.all_to_all(pieces, axis, split_axis=0, concat_axis=0, tiled=True)  39.5 us
    all_to_all x1, blocking collectives, local(): lax.all_to_all(sent, 'grp', split_axis=0, concat_axis=0, tiled=True)  18.6 us
    all_to_all x1, blocking collectives, local(): lax.all_to_all(line.reshape(high, part // high, width), 'blk_1', split_ax...  12.6 us
    all_to_all x1, blocking collectives, local(): lax.all_to_all(sent_back, 'grp', split_axis=0, concat_axis=0, tiled=True)  10.5 us
    pallas_call x5, Pallas kernels, call(): pl.pallas_call(body, name=name, in_specs=[smem] * len(scalars) + [anywher...  9.76 us
    ppermute x1, waiting for transfers between devices, local(): other = lax.ppermute(send, 'blk_2', swap)  2.25 us
  transfers between devices with their start and end apart: 1, of which 1 were waited for; matrix products, arithmetic and copies ran while one was open for 0% of the time, Pallas kernels for 0%

profile of v3, /device:TPU:2, one launch (start us, length us, event | category | flops | bytes accessed | tf_op | source)
XLA Modules:
  0.0 97.3 jit_solution(11402650455682073260)
XLA Ops:
  0.6 0.0 copy-start
  0.6 0.8 pad_add_fusion.scalar_ref
  1.4 3.2 %forward.1 = (f32[384,512]{1,0:T(8,128)S(1)}, f32[384,512]{1,0:T(8,128)S(1)}, f32[384,512]{1,0:T(8,128)S(1)}, f32[384,512]{1,0:T(8,128)S(1)}, bf16[4,128,512]{2,...) custom-call(s32[5]{0:T(128)S(1)} %pad_add_fusion.scalar_ref, ...), custom_call_target="tpu_custom_call" | custom-call | tf_op jit(solution)/shard_map/forward/pallas_call | solution.py:272
  4.7 18.6 %all_to_all.25.arrived_ref = bf16[4,128,512]{2,1,0:T(8,128)(2,1)S(1)} all-to-all(bf16[4,128,512]{2,1,0:T(8,128)(2,1)S(1)} %get-tuple-element.19), channel_id=1, replica_groups=mesh['grp'=4,'blk_0'=12,'blk_1'=8,'blk_2'=2] {'grp'}, dimensions={0} | all-to-all | bytes 1048576 | tf_op jit(solution)/shard_map/all_to_all | solution.py:305
  23.3 0.0 copy-done
  23.3 0.0 copy-start.1
  23.3 2.1 %middle.1 = (bf16[384,512]{1,0:T(8,128)(2,1)}, f32[384,512]{1,0:T(8,128)S(1)}, bf16[384,512]{1,0:T(8,128)(2,1)S(1)}, bf16[384,512]{1,0:T(8,128)(2,1)S(1)}, bf16[4,128,512]{2,1,0:T(8,128)(2,1)S(1)}) custom-call(s32[5]{0:T(128)S(1)} %pad_add_fusion.scalar_ref, f32[384,512]{1,0:T(8,128)S(1)} %get-tuple-element.18.second_ref, ...), custom_call_target="tpu_custom_call" | custom-call | tf_op jit(solution)/shard_map/middle/pallas_call | solution.py:272
  25.4 10.5 %all_to_all.26.arrived_ref = bf16[4,128,512]{2,1,0:T(8,128)(2,1)S(1)} all-to-all(bf16[4,128,512]{2,1,0:T(8,128)(2,1)S(1)} %get-tuple-element.23), channel_id=1, replica_groups=mesh['grp'=4,'blk_0'=12,'blk_1'=8,'blk_2'=2] {'grp'}, dimensions={0} | all-to-all | bytes 1048576 | tf_op jit(solution)/shard_map/all_to_all | solution.py:311
  35.9 0.0 copy-done.1
  35.9 4.1 %backward.1 = (bf16[384,512]{1,0:T(8,128)(2,1)}, bf16[3,256,512]{2,1,0:T(8,128)(2,1)S(1)}, bf16[3,256,512]{2,1,0:T(8,128)(2,1)S(1)}) custom-call(s32[5]{0:T(128)S(1)} %pad_add_fusion.scalar_ref, f32[384,512]{1,0:T(8,128)S(1)} %get-tuple-element.22.grad_summed_ref, bf16[4,128,512]{2,1,0:T(8,128)(2,1)S(1)} %all_to_all.26.arrived_ref, ...), custom_call_target="tpu_custom_call" | custom-call | tf_op jit(solution)/shard_map/backward/pallas_call | solution.py:272
  40.0 1.9 %collective-permute-start = (bf16[3,256,512]{2,1,0:T(8,128)(2,1)S(1)}, bf16[3,256,512]{2,1,0:T(8,128)(2,1)S(1)}, u32[]{:S(2)}, u32[]{:S(2)}) collective-permute-start(bf16[3,256,512]{2,1,0:T(8,128)(2,1)S(1)} %get-tuple-element.32), channel_id=1, source_target_pairs={{0,1},{1,0},{2,3},{3,2},{4,5},{5,4},{6,7},{7,6},{8,9},{9,8},{10,11... | collective-permute-start | bytes 2359304 | tf_op jit(solution)/shard_map/ppermute | solution.py:322
  42.0 2.3 %collective-permute-done.other_ref = bf16[3,256,512]{2,1,0:T(8,128)(2,1)S(1)} collective-permute-done((bf16[3,256,512]{2,1,0:T(8,128)(2,1)S(1)}, bf16[3,256,512]{2,1,0:T(8,128)(2,1)S(1)}, u32[]{:S(2)}, u32[]{:S(2)}) %collective-permute-start) | collective-permute-done | bytes 786464 | tf_op jit(solution)/shard_map/ppermute | solution.py:322
  44.2 0.2 join.1
  44.4 15.3 %all_to_all.27 = bf16[4,192,512]{2,1,0:T(8,128)(2,1)S(1)} all-to-all(bf16[4,192,512]{2,1,0:T(8,128)(2,1)S(1)} %join.1), channel_id=1, replica_groups=mesh['grp'=4,'blk_0'=12,'blk_1'=8,'blk_2'=2] {'grp'}, dimensions={0} | all-to-all | bytes 1572864 | tf_op jit(solution)/shard_map/all_to_all | solution.py:284
  59.7 0.1 reduce_sum.21
  59.8 12.6 %all_to_all.28.column_ref = bf16[8,24,512]{2,1,0:T(8,128)(2,1)S(1)} all-to-all(bf16[8,24,512]{2,1,0:T(8,128)(2,1)S(1)} %bitcast.6), channel_id=1, replica_groups=mesh['grp'=4,'blk_0'=12,'blk_1'=8,'blk_2'=2] {'blk_1'}, dimensions={0} | all-to-all | bytes 393216 | tf_op jit(solution)/shard_map/all_to_all | solution.py:330
  72.5 24.2 %all_to_all.29 = bf16[12,2,512]{2,1,0:T(2,128)(2,1)S(1)} all-to-all(bf16[12,2,512]{2,1,0:T(2,128)(2,1)S(1)} %plane.1), channel_id=1, replica_groups=mesh['grp'=4,'blk_0'=12,'blk_1'=8,'blk_2'=2] {'blk_0'}, dimensions={0} | all-to-all | bytes 49152 | tf_op jit(solution)/shard_map/all_to_all | solution.py:284
  96.7 0.6 broadcast_multiply_fusion
  (2 shorter events, 0.1 us)
Async XLA Ops:
  0.6 22.6 %copy-start = (bf16[384,512]{1,0:T(8,128)(2,1)S(1)}, bf16[384,512]{1,0:T(8,128)(2,1)}, u32[]{:S(2)}) copy-start(bf16[384,512]{1,0:T(8,128)(2,1)} %cotangent_ref.1) | copy-start | bytes 1179652
  23.3 12.6 %copy-start.1 = (s32[3,512]{1,0:T(4,128)S(1)}, s32[3,512]{1,0:T(4,128)}, u32[]{:S(2)}) copy-start(s32[3,512]{1,0:T(4,128)} %constant.17.clone.order_ref) | copy-start | bytes 18436
  40.0 4.2 %collective-permute-start = (bf16[3,256,512]{2,1,0:T(8,128)(2,1)S(1)}, bf16[3,256,512]{2,1,0:T(8,128)(2,1)S(1)}, u32[]{:S(2)}, u32[]{:S(2)}) collective-permute-start(bf16[3,256,512]{2,1,0:T(8,128)(2,1)S(1)} %get-tuple-element.32), channel_id=1, source_target_pairs={{0,1},{1,0},{2,3},{3,2},{4,5},{5,4},{6,7},{7,6},{8,9},{9,8},{10,11... | collective-permute-start | bytes 2359304 | tf_op jit(solution)/shard_map/ppermute | solution.py:322

commit v4 on v3

v4 whole, which is shorter than its diff:
```python
import math

import jax
import jax.numpy as jnp
from jax import lax
from jax.experimental import pallas as pl
from jax.experimental.pallas import tpu as pltpu
from jax.sharding import Mesh
from jax.sharding import PartitionSpec as P

NBR = 16
BLOCK = 128
GRP_BLK = ("grp", "blk_0", "blk_1", "blk_2")
BF16 = jnp.bfloat16
F32 = jnp.float32


def dot(a, b):
    return jnp.dot(a, b, preferred_element_type=F32)


def dot_nt(a, b):
    return lax.dot_general(a, b, (((1,), (1,)), ((), ())), preferred_element_type=F32)


def dot_tn(a, b):
    return lax.dot_general(a, b, (((0,), (0,)), ((), ())), preferred_element_type=F32)


def inverse_norm(hidden):
    return lax.rsqrt(jnp.mean(hidden * hidden, axis=-1, keepdims=True) + 1e-06)


def sigmoid(v):
    return 0.5 + 0.5 * jnp.tanh(0.5 * v)


def silu_slope(preact, sigma):
    return sigma * (1.0 + preact * (1.0 - sigma))


def layer_backward(unit, inverse, slope, weight, upstream):
    grad_pre = (upstream * slope).astype(BF16)
    grad_normed = dot_nt(grad_pre, weight)
    inner = jnp.mean(grad_normed * unit, axis=-1, keepdims=True)
    return upstream + inverse * (grad_normed - unit * inner), grad_pre


def basis_blocks(turned, atoms):
    pairs = NBR * NBR
    rows = atoms * NBR
    row = lax.broadcasted_iota(jnp.int32, (rows, atoms), 0)
    col = lax.broadcasted_iota(jnp.int32, (rows, atoms), 1)
    repeat = jnp.where(row // NBR == col, 1.0, 0.0).astype(BF16)
    wide = dot_nt(repeat, turned)
    row = lax.broadcasted_iota(jnp.int32, (rows, pairs), 0)
    col = lax.broadcasted_iota(jnp.int32, (rows, pairs), 1)
    wide = jnp.where(row % NBR == col // NBR, wide, 0.0).astype(BF16)
    row = lax.broadcasted_iota(jnp.int32, (pairs, BLOCK), 0)
    col = lax.broadcasted_iota(jnp.int32, (pairs, BLOCK), 1)
    tiled = dot(wide, jnp.where(row % NBR == col % NBR, 1.0, 0.0).astype(BF16))
    row = lax.broadcasted_iota(jnp.int32, (rows, BLOCK), 0)
    col = lax.broadcasted_iota(jnp.int32, (rows, BLOCK), 1)
    return jnp.where((row % BLOCK) // NBR == col // NBR, tiled, 0.0).astype(BF16)


def owner_of(number, count):
    owner = jnp.int32(0)
    for edge in range(1, 4):
        owner = owner + (number >= edge * count).astype(jnp.int32)
    return owner


def fill_slots(slots_ref, blocks_ref, partner_ref, group_count, count):
    owners = [owner_of(partner_ref[n], count) for n in range(count)]
    for d in range(group_count):
        pick = jnp.int32(0)
        for n in range(1, count):
            pick = jnp.where(owners[n] == d, n, pick)
        start = pl.multiple_of(pick * BLOCK, BLOCK)
        slots_ref[d] = blocks_ref[pl.ds(start, BLOCK), :]


def reverse_blocks(arrived_ref, own_ref, partner_ref, count):
    row = lax.broadcasted_iota(jnp.int32, (BLOCK, BLOCK), 0)
    col = lax.broadcasted_iota(jnp.int32, (BLOCK, BLOCK), 1)
    flip = jnp.where(row + 1 - 2 * (row % 2) == col, 1.0, 0.0).astype(BF16)
    picked = []
    for n in range(count):
        number = partner_ref[n]
        owner = owner_of(number, count)
        start = pl.multiple_of((number - owner * count) * BLOCK, BLOCK)
        near = own_ref[pl.ds(start, BLOCK), :].astype(BF16)
        picked.append(dot(flip, jnp.where(owner == lax.axis_index("grp"), near, arrived_ref[owner])))
    return jnp.concatenate(picked, axis=0)


def forward_body(partner_hbm, edge_hbm, turned_hbm, weight_hbm, unit_one_ref, inverse_one_ref,
                 normed_one_ref, slope_one_ref, unit_two_ref, inverse_two_ref, normed_two_ref,
                 slope_two_ref, second_ref, slots_ref, blocks_ref, weight_ref, partner_near_ref,
                 edge_ref, turned_ref, sent_ref, partner_ref, sems):
    rows = edge_ref.shape[0]
    count = rows // BLOCK
    turned_copy = pltpu.make_async_copy(turned_hbm, turned_ref, sems.at[0])
    edge_copy = pltpu.make_async_copy(edge_hbm, edge_ref, sems.at[1])
    weight_copies = [
        pltpu.make_async_copy(weight_hbm.at[n], weight_ref.at[n], sems.at[2 + n]) for n in range(3)
    ]
    partner_copies = [
        pltpu.make_async_copy(partner_hbm, partner_ref, sems.at[5]),
        pltpu.make_async_copy(partner_hbm, partner_near_ref, sems.at[6]),
    ]
    turned_copy.start()
    edge_copy.start()
    for copy in weight_copies + partner_copies:
        copy.start()
    turned_copy.wait()
    blocks_ref[...] = basis_blocks(turned_ref[...], rows // NBR)
    edge_copy.wait()
    mixed = jnp.concatenate(
        [
            dot(blocks_ref[n * BLOCK : (n + 1) * BLOCK, :], edge_ref[n * BLOCK : (n + 1) * BLOCK, :])
            for n in range(count)
        ],
        axis=0,
    )
    inverse = inverse_norm(mixed)
    unit = mixed * inverse
    normed = unit.astype(BF16)
    unit_one_ref[...] = unit
    inverse_one_ref[...] = inverse
    normed_one_ref[...] = normed
    weight_copies[0].wait()
    preact = dot(normed, weight_ref[0])
    sigma = sigmoid(preact)
    slope_one_ref[...] = silu_slope(preact, sigma)
    first = mixed + preact * sigma
    inverse = inverse_norm(first)
    unit = first * inverse
    normed = unit.astype(BF16)
    unit_two_ref[...] = unit
    inverse_two_ref[...] = inverse
    normed_two_ref[...] = normed
    weight_copies[1].wait()
    preact = dot(normed, weight_ref[1])
    sigma = sigmoid(preact)
    slope_two_ref[...] = silu_slope(preact, sigma)
    second = first + preact * sigma
    second_ref[...] = second
    sent_ref[...] = second.astype(BF16)
    for copy in partner_copies:
        copy.wait()
    fill_slots(slots_ref, sent_ref, partner_ref, slots_ref.shape[0], count)
    weight_copies[2].wait()


def middle_body(partner_ref, second_ref, arrived_ref, weight_ref, cotangent_ref, edge_out_hbm,
                grad_summed_ref, normed_ref, grad_pre_ref, slots_ref, sent_ref, edge_out_ref, sems):
    count = second_ref.shape[0] // BLOCK
    summed = second_ref[...] + reverse_blocks(arrived_ref, second_ref, partner_ref, count)
    inverse = inverse_norm(summed)
    unit = summed * inverse
    normed = unit.astype(BF16)
    normed_ref[...] = normed
    preact = dot(normed, weight_ref[2])
    sigma = sigmoid(preact)
    edge_out_ref[...] = (summed + preact * sigma).astype(BF16)
    copy = pltpu.make_async_copy(edge_out_ref, edge_out_hbm, sems.at[0])
    copy.start()
    grad_summed, grad_pre = layer_backward(
        unit, inverse, silu_slope(preact, sigma), weight_ref[2], cotangent_ref[...].astype(F32)
    )
    grad_pre_ref[...] = grad_pre
    grad_summed_ref[...] = grad_summed
    sent_ref[...] = grad_summed.astype(BF16)
    fill_slots(slots_ref, sent_ref, partner_ref, slots_ref.shape[0], count)
    copy.wait()


def split_by_core(grad_weight, tall_ref, keep_ref, send_ref, core):
    tiles, height, lanes = tall_ref.shape
    for t in range(tiles):
        tall_ref[t] = grad_weight[:, t * lanes : (t + 1) * lanes]
    for to_ref, side in ((keep_ref, core), (send_ref, 1 - core)):
        for i in range(2):
            for t in range(tiles):
                rows = tall_ref[t, pl.ds(2 * side + i, height // 4, stride=4), :]
                to_ref[i, :, t * lanes : (t + 1) * lanes] = rows.astype(BF16)


def backward_body(partner_ref, grad_summed_ref, arrived_ref, unit_one_ref, inverse_one_ref,
                  normed_one_ref, slope_one_ref, unit_two_ref, inverse_two_ref, normed_two_ref,
                  slope_two_ref, weight_ref, normed_three_ref, grad_pre_three_ref, keep_ref,
                  send_ref, grad_round_ref, tall_ref):
    count = unit_one_ref.shape[0] // BLOCK
    core = lax.axis_index("blk_2")
    grad_second = grad_summed_ref[...] + reverse_blocks(
        arrived_ref, grad_summed_ref, partner_ref, count
    )
    grad_first, grad_pre_two = layer_backward(
        unit_two_ref[...], inverse_two_ref[...], slope_two_ref[...], weight_ref[1], grad_second
    )
    grad_mixed, grad_pre_one = layer_backward(
        unit_one_ref[...], inverse_one_ref[...], slope_one_ref[...], weight_ref[0], grad_first
    )
    grad_round_ref[...] = grad_mixed.astype(BF16)
    pairs = (
        (normed_one_ref[...], grad_pre_one),
        (normed_two_ref[...], grad_pre_two),
        (normed_three_ref[...], grad_pre_three_ref[...]),
    )
    for layer, (normed, grad_pre) in enumerate(pairs):
        split_by_core(
            dot_tn(normed, grad_pre), tall_ref, keep_ref.at[layer], send_ref.at[layer], core
        )


def finish_body(grad_round_ref, blocks_ref, grad_state_hbm, grad_state_ref, sems):
    for n in range(grad_round_ref.shape[0] // BLOCK):
        rows = slice(n * BLOCK, (n + 1) * BLOCK)
        grad_state_ref[rows, :] = dot_tn(blocks_ref[rows, :], grad_round_ref[rows, :]).astype(BF16)
    copy = pltpu.make_async_copy(grad_state_ref, grad_state_hbm, sems.at[0])
    copy.start()
    copy.wait()


def join_body(keep_ref, other_ref, pair_ref):
    groups, _, part = pair_ref.shape[:3]
    height = keep_ref.shape[2]
    for layer in range(3):
        for i in range(2):
            rows = (keep_ref[layer, i].astype(F32) + other_ref[layer, i].astype(F32)).astype(BF16)
            done = 0
            while done < height:
                number = height * layer + done
                g, at = number // part, number % part
                size = min(height - done, part - at)
                pair_ref[g, i, at : at + size, :] = rows[done : done + size]
                done += size


def line_body(arrived_ref, line_ref, tall_ref, wide_ref):
    high, width = line_ref.shape[0], line_ref.shape[2]
    deep = line_ref.shape[1] // 2
    total = arrived_ref[0].astype(F32)
    for g in range(1, arrived_ref.shape[0]):
        total = total + arrived_ref[g].astype(F32)
    tiles, lanes = tall_ref.shape[0], tall_ref.shape[-1]
    for t in range(tiles):
        across = slice(t * lanes, (t + 1) * lanes)
        tall_ref[t] = total[:, :, across]
        for y in range(high):
            for i in range(2):
                wide_ref[t, y, pl.ds(i, deep, stride=2), :] = tall_ref[
                    t, i, pl.ds(y, deep, stride=high), :
                ]
        line_ref[:, :, across] = wide_ref[t].astype(BF16)


def plane_body(column_ref, plane_ref):
    total = column_ref[0].astype(F32)
    for y in range(1, column_ref.shape[0]):
        total = total + column_ref[y].astype(F32)
    deep, pair = plane_ref.shape[:2]
    for z in range(deep):
        plane_ref[z] = total[pair * z : pair * (z + 1)].astype(BF16)


def near(array):
    return pltpu.with_memory_space_constraint(array, pltpu.VMEM)


def away(array):
    return pltpu.with_memory_space_constraint(array, pltpu.HBM)


def call(body, name, scalars, far, arrays, far_outs, outs, scratch):
    smem = pl.BlockSpec(memory_space=pltpu.SMEM)
    vmem = pl.BlockSpec(memory_space=pltpu.VMEM)
    anywhere = pl.BlockSpec(memory_space=pltpu.HBM)
    return pl.pallas_call(
        body,
        name=name,
        in_specs=[smem] * len(scalars) + [anywhere] * len(far) + [vmem] * len(arrays),
        out_specs=[anywhere] * len(far_outs) + [vmem] * len(outs),
        out_shape=[jax.ShapeDtypeStruct(*o) for o in far_outs] + [pltpu.VMEM(*o) for o in outs],
        scratch_shapes=scratch,
        compiler_params=pltpu.CompilerParams(vmem_limit_bytes=24 * 1024 * 1024),
    )(*scalars, *[away(array) for array in far], *[near(array) for array in arrays])


def summed_over(pieces, axis):
    arrived = lax.all_to_all(pieces, axis, split_axis=0, concat_axis=0, tiled=True)
    return arrived.astype(F32).sum(axis=0)


def local(edge_state, basis, weights, partner, cotangent):
    rows, width = edge_state.shape
    groups, deep, high, cores = (lax.axis_size(a) for a in GRP_BLK)
    total_edges = rows * groups * deep * high * cores
    turned = basis.transpose(1, 2, 0).reshape(NBR * NBR, rows // NBR)
    full = ((rows, width), F32)
    half = ((rows, width), BF16)
    slots = ((groups, BLOCK, width), BF16)
    thin = ((rows, 1), F32)
    *saved, second, sent, blocks, weights_near, partner_near = call(
        forward_body, "forward", [], [partner, edge_state, turned, weights], [], [],
        [full, thin, half, full, full, thin, half, full, full, slots, ((rows, BLOCK), BF16),
         (weights.shape, BF16), (partner.shape, jnp.int32)],
        [pltpu.VMEM(*half), pltpu.VMEM(turned.shape, BF16), pltpu.VMEM(*half),
         pltpu.SMEM(partner.shape, jnp.int32), pltpu.SemaphoreType.DMA((7,))],
    )
    arrived = lax.all_to_all(sent, "grp", split_axis=0, concat_axis=0, tiled=True)
    edge_out, grad_summed, normed_three, grad_pre_three, sent_back = call(
        middle_body, "middle", [near(partner_near)], [], [second, arrived, weights_near, cotangent],
        [half], [full, half, half, slots],
        [pltpu.VMEM(*half), pltpu.VMEM(*half), pltpu.SemaphoreType.DMA((1,))],
    )
    returned = lax.all_to_all(sent_back, "grp", split_axis=0, concat_axis=0, tiled=True)
    swap = [(0, 1), (1, 0)]
    side = (3, 2, width // (2 * cores), width)
    keep, send, grad_round = call(
        backward_body, "backward", [near(partner_near)], [],
        [grad_summed, returned, *saved, weights_near, normed_three, grad_pre_three],
        [], [(side, BF16), (side, BF16), half], [pltpu.VMEM((width // 128, width, 128), F32)],
    )
    other = lax.ppermute(send, "blk_2", swap)
    (grad_state,) = call(
        finish_body, "finish", [], [], [grad_round, blocks], [half], [],
        [pltpu.VMEM(*half), pltpu.SemaphoreType.DMA((1,))],
    )
    part = 3 * width // (groups * cores)
    (pair,) = call(
        join_body, "join", [], [], [keep, other], [], [((groups, 2, part // 2, width), BF16)], [],
    )
    across = lax.all_to_all(pair, "grp", split_axis=0, concat_axis=0, tiled=True)
    (line,) = call(
        line_body, "line", [], [], [across], [], [((high, part // high, width), BF16)],
        [pltpu.VMEM((width // 128, 2, part // 2, 128), F32),
         pltpu.VMEM((width // 128, high, part // high, 128), F32)],
    )
    column = lax.all_to_all(
        line, "blk_1", split_axis=0, concat_axis=0, tiled=True
    )
    (plane,) = call(
        plane_body, "plane", [], [], [column], [],
        [((deep, part // high // deep, width), BF16)], [],
    )
    final = summed_over(plane, "blk_0")
    return edge_out, grad_state, final * (1.0 / math.sqrt(total_edges))


def solution(mesh):
    split = Mesh(mesh.devices.reshape(mesh.shape["grp"], 12, 8, 2), GRP_BLK)
    return jax.shard_map(
        local,
        mesh=split,
        in_specs=(P(GRP_BLK, None), P(GRP_BLK, None, None), P(), P(GRP_BLK), P(GRP_BLK, None)),
        out_specs=(P(GRP_BLK, None), P(GRP_BLK, None), P(GRP_BLK, None)),
        check_vma=False,
    )
```

time: 97.7 us -> 96.4 us (0.987)
  blocking collectives: 81.1 us -> 56.9 us
  starting transfers between devices: 1.92 us -> 15.9 us
  waiting for transfers between devices: 2.25 us -> 11.6 us
    all_to_all x3 -> x2, blocking collectives: 52.1 us -> 27.9 us  [the longest x1 15.3 us: local(): lax.all_to_all(pair, 'grp', split_axis=0, concat_axis=0, tiled=True)]
    all_to_all x0 -> x1, starting transfers between devices: none -> 14 us  [summed_over(): lax.all_to_all(pieces, axis, split_axis=0, concat_axis=0, tiled=True)]
    all_to_all x0 -> x1, waiting for transfers between devices: none -> 9.39 us  [summed_over(): lax.all_to_all(pieces, axis, split_axis=0, concat_axis=0, tiled=True)]
    pallas_call x5 -> x7, Pallas kernels: 9.76 us -> 10.2 us  [call(): pl.pallas_call(body, name=name, in_specs=[smem] * len(scalars) + [anywher...]
  transfers between devices with their start and end apart: 1 -> 2, of which waited for: 1 -> 2; matrix products, arithmetic and copies ran while one was open for 0% -> 0% of each run, Pallas kernels for 0% -> 1%
where the time goes in v4:
time: 96.4 us; the launch traced here: 96.1 us
  blocking collectives  56.9 us (59%)
  starting transfers between devices  15.9 us (16%)
  waiting for transfers between devices  11.6 us (12%)
  Pallas kernels  10.2 us (11%)
    all_to_all x1, blocking collectives, local(): lax.all_to_all(sent, 'grp', split_axis=0, concat_axis=0, tiled=True)  18.6 us
    all_to_all x1, blocking collectives, local(): lax.all_to_all(pair, 'grp', split_axis=0, concat_axis=0, tiled=True)  15.3 us
    all_to_all x1, starting transfers between devices, summed_over(): lax.all_to_all(pieces, axis, split_axis=0, concat_axis=0, tiled=True)  14 us
    all_to_all x1, blocking collectives, local(): lax.all_to_all(line, 'blk_1', split_axis=0, concat_axis=0, tiled=True)  12.6 us
    all_to_all x1, blocking collectives, local(): lax.all_to_all(sent_back, 'grp', split_axis=0, concat_axis=0, tiled=True)  10.5 us
    pallas_call x7, Pallas kernels, call(): pl.pallas_call(body, name=name, in_specs=[smem] * len(scalars) + [anywher...  10.2 us
    all_to_all x1, waiting for transfers between devices, summed_over(): lax.all_to_all(pieces, axis, split_axis=0, concat_axis=0, tiled=True)  9.39 us
    ppermute x1, waiting for transfers between devices, local(): other = lax.ppermute(send, 'blk_2', swap)  2.25 us
  transfers between devices with their start and end apart: 2, of which 2 were waited for; matrix products, arithmetic and copies ran while one was open for 0% of the time, Pallas kernels for 1%

profile of v4, /device:TPU:2, one launch (start us, length us, event | category | flops | bytes accessed | tf_op | source)
XLA Modules:
  0.0 96.1 jit_solution(7132886240874228746)
XLA Ops:
  0.6 0.0 copy-start
  0.6 3.0 %forward.1 = (f32[384,512]{1,0:T(8,128)S(1)}, f32[384,1]{1,0:T(8,128)S(1)}, bf16[384,512]{1,0:T(8,128)(2,1)S(1)}, f32[384,512]{1,0:T(8,128)S(1)}, f32[384,512]{1...) custom-call(s32[3]{0:T(128)} %partner_hbm.1, ...), custom_call_target="tpu_custom_call" | custom-call | tf_op jit(solution)/shard_map/forward/pallas_call | solution.py:281
  3.7 18.6 %all_to_all.25.arrived_ref = bf16[4,128,512]{2,1,0:T(8,128)(2,1)S(1)} all-to-all(bf16[4,128,512]{2,1,0:T(8,128)(2,1)S(1)} %get-tuple-element.26), channel_id=1, replica_groups=mesh['grp'=4,'blk_0'=12,'blk_1'=8,'blk_2'=2] {'grp'}, dimensions={0} | all-to-all | bytes 1048576 | tf_op jit(solution)/shard_map/all_to_all | solution.py:313
  22.2 0.0 copy-done
  22.2 2.2 %middle.1 = (bf16[384,512]{1,0:T(8,128)(2,1)}, f32[384,512]{1,0:T(8,128)S(1)}, bf16[384,512]{1,0:T(8,128)(2,1)S(1)}, bf16[384,512]{1,0:T(8,128)(2,1)S(1)}, bf16[4,128,512]{2,1,0:T(8,128)(2,1)S(1)}) custom-call(s32[3]{0:T(128)S(1)} %get-tuple-element.24.partner_ref, f32[384,512]{1,0:T(8,128)S(1)} %get-tuple-element.25.second_ref, ...), custom_call_target="tpu_custom_call" | custom-call | tf_op jit(solution)/shard_map/middle/pallas_call | solution.py:281
  24.4 10.5 %all_to_all.26.arrived_ref = bf16[4,128,512]{2,1,0:T(8,128)(2,1)S(1)} all-to-all(bf16[4,128,512]{2,1,0:T(8,128)(2,1)S(1)} %get-tuple-element.30), channel_id=1, replica_groups=mesh['grp'=4,'blk_0'=12,'blk_1'=8,'blk_2'=2] {'grp'}, dimensions={0} | all-to-all | bytes 1048576 | tf_op jit(solution)/shard_map/all_to_all | solution.py:319
  34.9 2.9 %backward.1 = (bf16[3,2,128,512]{3,2,1,0:T(8,128)(2,1)S(1)}, bf16[3,2,128,512]{3,2,1,0:T(8,128)(2,1)S(1)}, bf16[384,512]{1,0:T(8,128)(2,1)S(1)}) custom-call(s32[3]{0:T(128)S(1)} %get-tuple-element.24.partner_ref, f32[384,512]{1,0:T(8,128)S(1)} %get-tuple-element.29.grad_summed_ref, bf16[4,128,512]{2,1,0:T(8,128)(2,1)S(1)} %all_to_all.26.arrived_ref, ...), custom_call_target="tpu_custom_call" | custom-call | tf_op jit(solution)/shard_map/backward/pallas_call | solution.py:281
  37.8 1.9 %collective-permute-start = (bf16[3,2,128,512]{3,2,1,0:T(8,128)(2,1)S(1)}, bf16[3,2,128,512]{3,2,1,0:T(8,128)(2,1)S(1)}, u32[]{:S(2)}, u32[]{:S(2)}) collective-permute-start(bf16[3,2,128,512]{3,2,1,0:T(8,128)(2,1)S(1)} %get-tuple-element.44), channel_id=1, source_target_pairs={{0,1},{1,0},{2,3},{3,2},{4,5},{5,4},{6,7},{7,6},{8,9},{9,8},{10,11... | collective-permute-start | bytes 2359304 | tf_op jit(solution)/shard_map/ppermute | solution.py:327
  39.8 2.3 %collective-permute-done.other_ref = bf16[3,2,128,512]{3,2,1,0:T(8,128)(2,1)S(1)} collective-permute-done((bf16[3,2,128,512]{3,2,1,0:T(8,128)(2,1)S(1)}, bf16[3,2,128,512]{3,2,1,0:T(8,128)(2,1)S(1)}, u32[]{:S(2)}, u32[]{:S(2)}) %collective-permute-start) | collective-permute-done | bytes 786464 | tf_op jit(solution)/shard_map/ppermute | solution.py:327
  42.0 0.2 join.1
  42.2 15.3 %all_to_all.27.arrived_ref = bf16[4,2,96,512]{3,2,1,0:T(8,128)(2,1)S(1)} all-to-all(bf16[4,2,96,512]{3,2,1,0:T(8,128)(2,1)S(1)} %join.1), channel_id=1, replica_groups=mesh['grp'=4,'blk_0'=12,'blk_1'=8,'blk_2'=2] {'grp'}, dimensions={0} | all-to-all | bytes 1572864 | tf_op jit(solution)/shard_map/all_to_all | solution.py:336
  57.5 0.3 line.1
  57.7 12.6 %all_to_all.28.column_ref = bf16[8,24,512]{2,1,0:T(8,128)(2,1)S(1)} all-to-all(bf16[8,24,512]{2,1,0:T(8,128)(2,1)S(1)} %line.1), channel_id=1, replica_groups=mesh['grp'=4,'blk_0'=12,'blk_1'=8,'blk_2'=2] {'blk_1'}, dimensions={0} | all-to-all | bytes 393216 | tf_op jit(solution)/shard_map/all_to_all | solution.py:342
  70.3 0.6 plane.1
  71.0 14.0 %all-to-all-start.4 = ((bf16[12,2,512]{2,1,0:T(2,128)(2,1)}), bf16[12,2,512]{2,1,0:T(2,128)(2,1)S(1)}, u32[]{:S(2)}, u32[]{:S(2)}) async-start(bf16[12,2,512]{2,1,0:T(2,128)(2,1)} %plane.1), calls=%async_computation.4 | async-start | bytes 49152 | tf_op jit(solution)/shard_map/all_to_all | solution.py:293
  85.0 1.0 %finish.1 = bf16[384,512]{1,0:T(8,128)(2,1)} custom-call(bf16[384,512]{1,0:T(8,128)(2,1)S(1)} %get-tuple-element.41.grad_round_ref, bf16[384,128]{1,0:T(8,128)(2,1)S(1)} %get-tuple-element.42.blocks_ref), custom_call_target="tpu_custom_call" | custom-call | tf_op jit(solution)/shard_map/finish/pallas_call | solution.py:281
  86.0 9.4 %all-to-all-done.4 = bf16[12,2,512]{2,1,0:T(2,128)(2,1)S(1)} async-done(((bf16[12,2,512]{2,1,0:T(2,128)(2,1)}), bf16[12,2,512]{2,1,0:T(2,128)(2,1)S(1)}, u32[]{:S(2)}, u32[]{:S(2)}) %all-to-all-start.4) | async-done | bytes 24608 | tf_op jit(solution)/shard_map/all_to_all | solution.py:293
  95.5 0.6 broadcast_multiply_fusion
  (1 shorter events, 0.0 us)
Async XLA Ops:
  0.6 21.6 %copy-start = (bf16[384,512]{1,0:T(8,128)(2,1)S(1)}, bf16[384,512]{1,0:T(8,128)(2,1)}, u32[]{:S(2)}) copy-start(bf16[384,512]{1,0:T(8,128)(2,1)} %cotangent_ref.1) | copy-start | bytes 1179652
  37.8 4.2 %collective-permute-start = (bf16[3,2,128,512]{3,2,1,0:T(8,128)(2,1)S(1)}, bf16[3,2,128,512]{3,2,1,0:T(8,128)(2,1)S(1)}, u32[]{:S(2)}, u32[]{:S(2)}) collective-permute-start(bf16[3,2,128,512]{3,2,1,0:T(8,128)(2,1)S(1)} %get-tuple-element.44), channel_id=1, source_target_pairs={{0,1},{1,0},{2,3},{3,2},{4,5},{5,4},{6,7},{7,6},{8,9},{9,8},{10,11... | collective-permute-start | bytes 2359304 | tf_op jit(solution)/shard_map/ppermute | solution.py:327
  71.0 24.5 %all-to-all-start.4 = ((bf16[12,2,512]{2,1,0:T(2,128)(2,1)}), bf16[12,2,512]{2,1,0:T(2,128)(2,1)S(1)}, u32[]{:S(2)}, u32[]{:S(2)}) async-start(bf16[12,2,512]{2,1,0:T(2,128)(2,1)} %plane.1), calls=%async_computation.4 | async-start | bytes 49152 | tf_op jit(solution)/shard_map/all_to_all | solution.py:293

commit v5 on v4

--- a/solution.py
+++ b/solution.py
@@ -71,33 +71,38 @@
     return owner
 
 
-def fill_slots(slots_ref, blocks_ref, partner_ref, group_count, count):
+def fill_slots(slots_ref, sources, partner_ref, count):
     owners = [owner_of(partner_ref[n], count) for n in range(count)]
-    for d in range(group_count):
+    for d in range(slots_ref.shape[0]):
         pick = jnp.int32(0)
         for n in range(1, count):
             pick = jnp.where(owners[n] == d, n, pick)
         start = pl.multiple_of(pick * BLOCK, BLOCK)
-        slots_ref[d] = blocks_ref[pl.ds(start, BLOCK), :]
-
-
-def reverse_blocks(arrived_ref, own_ref, partner_ref, count):
+        for at, source_ref in enumerate(sources):
+            slots_ref[d, at * BLOCK : (at + 1) * BLOCK, :] = source_ref[pl.ds(start, BLOCK), :]
+
+
+def reversed_blocks(arrived_ref, sources, partner_ref, count):
     row = lax.broadcasted_iota(jnp.int32, (BLOCK, BLOCK), 0)
     col = lax.broadcasted_iota(jnp.int32, (BLOCK, BLOCK), 1)
     flip = jnp.where(row + 1 - 2 * (row % 2) == col, 1.0, 0.0).astype(BF16)
-    picked = []
+    own = lax.axis_index("grp")
+    picked = [[] for _ in sources]
     for n in range(count):
         number = partner_ref[n]
         owner = owner_of(number, count)
         start = pl.multiple_of((number - owner * count) * BLOCK, BLOCK)
-        near = own_ref[pl.ds(start, BLOCK), :].astype(BF16)
-        picked.append(dot(flip, jnp.where(owner == lax.axis_index("grp"), near, arrived_ref[owner])))
-    return jnp.concatenate(picked, axis=0)
-
-
-def forward_body(partner_hbm, edge_hbm, turned_hbm, weight_hbm, unit_one_ref, inverse_one_ref,
+        for at, source_ref in enumerate(sources):
+            near = source_ref[pl.ds(start, BLOCK), :].astype(BF16)
+            far = arrived_ref[owner, at * BLOCK : (at + 1) * BLOCK, :]
+            picked[at].append(dot(flip, jnp.where(owner == own, near, far)))
+    return [jnp.concatenate(blocks, axis=0) for blocks in picked]
+
+
+def forward_body(partner_hbm, edge_hbm, turned_hbm, weight_hbm, cotangent_hbm, unit_one_ref, inverse_one_ref,
                  normed_one_ref, slope_one_ref, unit_two_ref, inverse_two_ref, normed_two_ref,
                  slope_two_ref, second_ref, slots_ref, blocks_ref, weight_ref, partner_near_ref,
+                 cotangent_ref,
                  edge_ref, turned_ref, sent_ref, partner_ref, sems):
     rows = edge_ref.shape[0]
     count = rows // BLOCK
@@ -109,6 +114,7 @@
     partner_copies = [
         pltpu.make_async_copy(partner_hbm, partner_ref, sems.at[5]),
         pltpu.make_async_copy(partner_hbm, partner_near_ref, sems.at[6]),
+        pltpu.make_async_copy(cotangent_hbm, cotangent_ref, sems.at[7]),
     ]
     turned_copy.start()
     edge_copy.start()
@@ -150,31 +156,8 @@
     sent_ref[...] = second.astype(BF16)
     for copy in partner_copies:
         copy.wait()
-    fill_slots(slots_ref, sent_ref, partner_ref, slots_ref.shape[0], count)
+    fill_slots(slots_ref, (sent_ref, cotangent_ref), partner_ref, count)
     weight_copies[2].wait()
-
-
-def middle_body(partner_ref, second_ref, arrived_ref, weight_ref, cotangent_ref, edge_out_hbm,
-                grad_summed_ref, normed_ref, grad_pre_ref, slots_ref, sent_ref, edge_out_ref, sems):
-    count = second_ref.shape[0] // BLOCK
-    summed = second_ref[...] + reverse_blocks(arrived_ref, second_ref, partner_ref, count)
-    inverse = inverse_norm(summed)
-    unit = summed * inverse
-    normed = unit.astype(BF16)
-    normed_ref[...] = normed
-    preact = dot(normed, weight_ref[2])
-    sigma = sigmoid(preact)
-    edge_out_ref[...] = (summed + preact * sigma).astype(BF16)
-    copy = pltpu.make_async_copy(edge_out_ref, edge_out_hbm, sems.at[0])
-    copy.start()
-    grad_summed, grad_pre = layer_backward(
-        unit, inverse, silu_slope(preact, sigma), weight_ref[2], cotangent_ref[...].astype(F32)
-    )
-    grad_pre_ref[...] = grad_pre
-    grad_summed_ref[...] = grad_summed
-    sent_ref[...] = grad_summed.astype(BF16)
-    fill_slots(slots_ref, sent_ref, partner_ref, slots_ref.shape[0], count)
-    copy.wait()
 
 
 def split_by_core(grad_weight, tall_ref, keep_ref, send_ref, core):
@@ -188,15 +171,30 @@
                 to_ref[i, :, t * lanes : (t + 1) * lanes] = rows.astype(BF16)
 
 
-def backward_body(partner_ref, grad_summed_ref, arrived_ref, unit_one_ref, inverse_one_ref,
-                  normed_one_ref, slope_one_ref, unit_two_ref, inverse_two_ref, normed_two_ref,
-                  slope_two_ref, weight_ref, normed_three_ref, grad_pre_three_ref, keep_ref,
-                  send_ref, grad_round_ref, tall_ref):
-    count = unit_one_ref.shape[0] // BLOCK
+def backward_body(partner_ref, second_ref, cotangent_ref, arrived_ref, unit_one_ref,
+                  inverse_one_ref, normed_one_ref, slope_one_ref, unit_two_ref, inverse_two_ref,
+                  normed_two_ref, slope_two_ref, weight_ref, edge_out_hbm, keep_ref, send_ref,
+                  grad_round_ref, edge_out_ref, tall_ref, sems):
+    rows = second_ref.shape[0]
     core = lax.axis_index("blk_2")
-    grad_second = grad_summed_ref[...] + reverse_blocks(
-        arrived_ref, grad_summed_ref, partner_ref, count
-    )
+    other, other_cotangent = reversed_blocks(
+        arrived_ref, (second_ref, cotangent_ref), partner_ref, rows // BLOCK
+    )
+    second = second_ref[...]
+    summed = jnp.concatenate([second + other, other + second.astype(BF16).astype(F32)], axis=0)
+    upstream = jnp.concatenate([cotangent_ref[...].astype(F32), other_cotangent], axis=0)
+    inverse = inverse_norm(summed)
+    unit = summed * inverse
+    normed = unit.astype(BF16)
+    preact = dot(normed, weight_ref[2])
+    sigma = sigmoid(preact)
+    edge_out_ref[...] = (summed[:rows] + preact[:rows] * sigma[:rows]).astype(BF16)
+    copy = pltpu.make_async_copy(edge_out_ref, edge_out_hbm, sems.at[0])
+    copy.start()
+    grad_summed, grad_pre_three = layer_backward(
+        unit, inverse, silu_slope(preact, sigma), weight_ref[2], upstream
+    )
+    grad_second = grad_summed[:rows] + grad_summed[rows:].astype(BF16).astype(F32)
     grad_first, grad_pre_two = layer_backward(
         unit_two_ref[...], inverse_two_ref[...], slope_two_ref[...], weight_ref[1], grad_second
     )
@@ -207,24 +205,26 @@
     pairs = (
         (normed_one_ref[...], grad_pre_one),
         (normed_two_ref[...], grad_pre_two),
-        (normed_three_ref[...], grad_pre_three_ref[...]),
+        (normed[:rows], grad_pre_three[:rows]),
     )
     for layer, (normed, grad_pre) in enumerate(pairs):
         split_by_core(
             dot_tn(normed, grad_pre), tall_ref, keep_ref.at[layer], send_ref.at[layer], core
         )
-
-
-def finish_body(grad_round_ref, blocks_ref, grad_state_hbm, grad_state_ref, sems):
+    copy.wait()
+
+
+def finish_body(grad_round_ref, blocks_ref, grad_state_hbm, token_ref, grad_state_ref, sems):
     for n in range(grad_round_ref.shape[0] // BLOCK):
         rows = slice(n * BLOCK, (n + 1) * BLOCK)
         grad_state_ref[rows, :] = dot_tn(blocks_ref[rows, :], grad_round_ref[rows, :]).astype(BF16)
     copy = pltpu.make_async_copy(grad_state_ref, grad_state_hbm, sems.at[0])
     copy.start()
+    token_ref[...] = jnp.zeros_like(token_ref)
     copy.wait()
 
 
-def join_body(keep_ref, other_ref, pair_ref):
+def join_body(keep_ref, other_ref, token_ref, pair_ref):
     groups, _, part = pair_ref.shape[:3]
     height = keep_ref.shape[2]
     for layer in range(3):
@@ -301,37 +301,34 @@
     turned = basis.transpose(1, 2, 0).reshape(NBR * NBR, rows // NBR)
     full = ((rows, width), F32)
     half = ((rows, width), BF16)
-    slots = ((groups, BLOCK, width), BF16)
+    slots = ((groups, 2 * BLOCK, width), BF16)
     thin = ((rows, 1), F32)
-    *saved, second, sent, blocks, weights_near, partner_near = call(
-        forward_body, "forward", [], [partner, edge_state, turned, weights], [], [],
+    *saved, second, sent, blocks, weights_near, partner_near, cotangent_near = call(
+        forward_body, "forward", [], [partner, edge_state, turned, weights, cotangent],
+        [], [],
         [full, thin, half, full, full, thin, half, full, full, slots, ((rows, BLOCK), BF16),
-         (weights.shape, BF16), (partner.shape, jnp.int32)],
+         (weights.shape, BF16), (partner.shape, jnp.int32), half],
         [pltpu.VMEM(*half), pltpu.VMEM(turned.shape, BF16), pltpu.VMEM(*half),
-         pltpu.SMEM(partner.shape, jnp.int32), pltpu.SemaphoreType.DMA((7,))],
+         pltpu.SMEM(partner.shape, jnp.int32), pltpu.SemaphoreType.DMA((8,))],
     )
     arrived = lax.all_to_all(sent, "grp", split_axis=0, concat_axis=0, tiled=True)
-    edge_out, grad_summed, normed_three, grad_pre_three, sent_back = call(
-        middle_body, "middle", [near(partner_near)], [], [second, arrived, weights_near, cotangent],
-        [half], [full, half, half, slots],
-        [pltpu.VMEM(*half), pltpu.VMEM(*half), pltpu.SemaphoreType.DMA((1,))],
-    )
-    returned = lax.all_to_all(sent_back, "grp", split_axis=0, concat_axis=0, tiled=True)
     swap = [(0, 1), (1, 0)]
     side = (3, 2, width // (2 * cores), width)
-    keep, send, grad_round = call(
+    edge_out, keep, send, grad_round = call(
         backward_body, "backward", [near(partner_near)], [],
-        [grad_summed, returned, *saved, weights_near, normed_three, grad_pre_three],
-        [], [(side, BF16), (side, BF16), half], [pltpu.VMEM((width // 128, width, 128), F32)],
+        [second, cotangent_near, arrived, *saved, weights_near],
+        [half], [(side, BF16), (side, BF16), half],
+        [pltpu.VMEM(*half), pltpu.VMEM((width // 128, width, 128), F32),
+         pltpu.SemaphoreType.DMA((1,))],
     )
     other = lax.ppermute(send, "blk_2", swap)
-    (grad_state,) = call(
-        finish_body, "finish", [], [], [grad_round, blocks], [half], [],
+    grad_state, token = call(
+        finish_body, "finish", [], [], [grad_round, blocks], [half], [((8, 128), F32)],
         [pltpu.VMEM(*half), pltpu.SemaphoreType.DMA((1,))],
     )
     part = 3 * width // (groups * cores)
     (pair,) = call(
-        join_body, "join", [], [], [keep, other], [], [((groups, 2, part // 2, width), BF16)], [],
+        join_body, "join", [], [], [keep, other, token], [], [((groups, 2, part // 2, width), BF16)], [],
     )
     across = lax.all_to_all(pair, "grp", split_axis=0, concat_axis=0, tiled=True)
     (line,) = call(

time: 96.4 us -> 89.6 us (0.929)
  blocking collectives: 56.9 us -> 75.8 us
  starting transfers between devices: 15.9 us -> 1.92 us
  waiting for transfers between devices: 11.6 us -> 1.2 us
  Pallas kernels: 10.2 us -> 9.1 us
    all_to_all x1, blocking collectives: 10.5 us -> 25.4 us  [summed_over(): lax.all_to_all(pieces, axis, split_axis=0, concat_axis=0, tiled=True)]
    all_to_all x1 -> x0, starting transfers between devices: 14 us -> none  [summed_over(): lax.all_to_all(pieces, axis, split_axis=0, concat_axis=0, tiled=True)]
    all_to_all x1 -> x0, waiting for transfers between devices: 9.39 us -> none  [summed_over(): lax.all_to_all(pieces, axis, split_axis=0, concat_axis=0, tiled=True)]
    all_to_all x1, blocking collectives: 18.6 us -> 21.4 us  [local(): lax.all_to_all(sent, 'grp', split_axis=0, concat_axis=0, tiled=True)]
    pallas_call x7 -> x6, Pallas kernels: 10.2 us -> 9.1 us  [call(): pl.pallas_call(body, name=name, in_specs=[smem] * len(scalars) + [anywher...]
    all_to_all x1, blocking collectives: 12.6 us -> 13.7 us  [local(): lax.all_to_all(line, 'blk_1', split_axis=0, concat_axis=0, tiled=True)]
    ppermute x1, waiting for transfers between devices: 2.25 us -> 1.2 us  [local(): other = lax.ppermute(send, 'blk_2', swap)]
  transfers between devices with their start and end apart: 2 -> 1, of which waited for: 2 -> 1; matrix products, arithmetic and copies ran while one was open for 0% -> 0% of each run, Pallas kernels for 1% -> 1%
where the time goes in v5:
time: 89.6 us; the launch traced here: 89.3 us
  blocking collectives  75.8 us (85%)
  Pallas kernels  9.1 us (10%)
  starting transfers between devices  1.92 us (2%)
  waiting for transfers between devices  1.2 us (1%)
    all_to_all x1, blocking collectives, summed_over(): lax.all_to_all(pieces, axis, split_axis=0, concat_axis=0, tiled=True)  25.4 us
    all_to_all x1, blocking collectives, local(): lax.all_to_all(sent, 'grp', split_axis=0, concat_axis=0, tiled=True)  21.4 us
    all_to_all x1, blocking collectives, local(): lax.all_to_all(pair, 'grp', split_axis=0, concat_axis=0, tiled=True)  15.3 us
    all_to_all x1, blocking collectives, local(): lax.all_to_all(line, 'blk_1', split_axis=0, concat_axis=0, tiled=True)  13.7 us
    pallas_call x6, Pallas kernels, call(): pl.pallas_call(body, name=name, in_specs=[smem] * len(scalars) + [anywher...  9.1 us
    ppermute x1, starting transfers between devices, local(): other = lax.ppermute(send, 'blk_2', swap)  1.92 us
  transfers between devices with their start and end apart: 1, of which 1 were waited for; matrix products, arithmetic and copies ran while one was open for 0% of the time, Pallas kernels for 1%

profile of v5, /device:TPU:2, one launch (start us, length us, event | category | flops | bytes accessed | tf_op | source)
XLA Modules:
  0.0 89.3 jit_solution(16162810120287446070)
XLA Ops:
  0.6 3.0 %forward.1 = (f32[384,512]{1,0:T(8,128)S(1)}, f32[384,1]{1,0:T(8,128)S(1)}, bf16[384,512]{1,0:T(8,128)(2,1)S(1)}, f32[384,512]{1,0:T(8,128)S(1)}, f32[384,512]{1...) custom-call(s32[3]{0:T(128)} %partner_hbm.1, ...), custom_call_target="tpu_custom_call" | custom-call | tf_op jit(solution)/shard_map/forward/pallas_call | solution.py:281
  3.6 21.4 %all_to_all.20.arrived_ref = bf16[4,256,512]{2,1,0:T(8,128)(2,1)S(1)} all-to-all(bf16[4,256,512]{2,1,0:T(8,128)(2,1)S(1)} %get-tuple-element.26), channel_id=1, replica_groups=mesh['grp'=4,'blk_0'=12,'blk_1'=8,'blk_2'=2] {'grp'}, dimensions={0} | all-to-all | bytes 2097152 | tf_op jit(solution)/shard_map/all_to_all | solution.py:314
  25.0 4.6 %backward.1 = (bf16[384,512]{1,0:T(8,128)(2,1)}, bf16[3,2,128,512]{3,2,1,0:T(8,128)(2,1)S(1)}, bf16[3,2,128,512]{3,2,1,0:T(8,128)(2,1)S(1)}, bf16[384,512]{1,0:T(8,128)(2,1)S(1)}) custom-call(s32[3]{0:T(128)S(1)} %get-tuple-element.23.partner_ref, f32[384,512]{1,0:T(8,128)S(1)} %get-tuple-element.24.second_ref, ...), custom_call_target="tpu_custom_call" | custom-call | tf_op jit(solution)/shard_map/backward/pallas_call | solution.py:281
  29.6 1.9 %collective-permute-start = (bf16[3,2,128,512]{3,2,1,0:T(8,128)(2,1)S(1)}, bf16[3,2,128,512]{3,2,1,0:T(8,128)(2,1)S(1)}, u32[]{:S(2)}, u32[]{:S(2)}) collective-permute-start(bf16[3,2,128,512]{3,2,1,0:T(8,128)(2,1)S(1)} %get-tuple-element.41), channel_id=1, source_target_pairs={{0,1},{1,0},{2,3},{3,2},{4,5},{5,4},{6,7},{7,6},{8,9},{9,8},{10,11... | collective-permute-start | bytes 2359304 | tf_op jit(solution)/shard_map/ppermute | solution.py:324
  31.5 1.0 %finish.1 = (bf16[384,512]{1,0:T(8,128)(2,1)}, f32[8,128]{1,0:T(8,128)S(1)}) custom-call(bf16[384,512]{1,0:T(8,128)(2,1)S(1)} %get-tuple-element.37.grad_round_ref, bf16[384,128]{1,0:T(8,128)(2,1)S(1)} %get-tuple-element.38.blocks_ref), custom_call_target="tpu_custom_call" | custom-call | tf_op jit(solution)/shard_map/finish/pallas_call | solution.py:281
  32.6 1.2 %collective-permute-done.other_ref = bf16[3,2,128,512]{3,2,1,0:T(8,128)(2,1)S(1)} collective-permute-done((bf16[3,2,128,512]{3,2,1,0:T(8,128)(2,1)S(1)}, bf16[3,2,128,512]{3,2,1,0:T(8,128)(2,1)S(1)}, u32[]{:S(2)}, u32[]{:S(2)}) %collective-permute-start) | collective-permute-done | bytes 786464 | tf_op jit(solution)/shard_map/ppermute | solution.py:324
  33.8 0.2 join.1
  34.0 15.3 %all_to_all.21.arrived_ref = bf16[4,2,96,512]{3,2,1,0:T(8,128)(2,1)S(1)} all-to-all(bf16[4,2,96,512]{3,2,1,0:T(8,128)(2,1)S(1)} %join.1), channel_id=1, replica_groups=mesh['grp'=4,'blk_0'=12,'blk_1'=8,'blk_2'=2] {'grp'}, dimensions={0} | all-to-all | bytes 1572864 | tf_op jit(solution)/shard_map/all_to_all | solution.py:333
  49.3 0.3 line.1
  49.5 13.7 %all_to_all.22.column_ref = bf16[8,24,512]{2,1,0:T(8,128)(2,1)S(1)} all-to-all(bf16[8,24,512]{2,1,0:T(8,128)(2,1)S(1)} %line.1), channel_id=1, replica_groups=mesh['grp'=4,'blk_0'=12,'blk_1'=8,'blk_2'=2] {'blk_1'}, dimensions={0} | all-to-all | bytes 393216 | tf_op jit(solution)/shard_map/all_to_all | solution.py:339
  63.3 25.4 %all_to_all.23 = bf16[12,2,512]{2,1,0:T(2,128)(2,1)S(1)} all-to-all(bf16[12,2,512]{2,1,0:T(2,128)(2,1)S(1)} %plane.1), channel_id=1, replica_groups=mesh['grp'=4,'blk_0'=12,'blk_1'=8,'blk_2'=2] {'blk_0'}, dimensions={0} | all-to-all | bytes 49152 | tf_op jit(solution)/shard_map/all_to_all | solution.py:293
  88.7 0.6 broadcast_multiply_fusion
  (2 shorter events, 0.1 us)
Async XLA Ops:
  29.6 4.2 %collective-permute-start = (bf16[3,2,128,512]{3,2,1,0:T(8,128)(2,1)S(1)}, bf16[3,2,128,512]{3,2,1,0:T(8,128)(2,1)S(1)}, u32[]{:S(2)}, u32[]{:S(2)}) collective-permute-start(bf16[3,2,128,512]{3,2,1,0:T(8,128)(2,1)S(1)} %get-tuple-element.41), channel_id=1, source_target_pairs={{0,1},{1,0},{2,3},{3,2},{4,5},{5,4},{6,7},{7,6},{8,9},{9,8},{10,11... | collective-permute-start | bytes 2359304 | tf_op jit(solution)/shard_map/ppermute | solution.py:324

commit v6 on v5

--- a/solution.py
+++ b/solution.py
@@ -35,8 +35,8 @@
     return 0.5 + 0.5 * jnp.tanh(0.5 * v)
 
 
-def silu_slope(preact, sigma):
-    return sigma * (1.0 + preact * (1.0 - sigma))
+def silu_slope(gated, sigma):
+    return sigma + gated * (1.0 - sigma)
 
 
 def layer_backward(unit, inverse, slope, weight, upstream):
@@ -46,19 +46,25 @@
     return upstream + inverse * (grad_normed - unit * inner), grad_pre
 
 
-def basis_blocks(turned, atoms):
+def basis_choices(atoms):
     pairs = NBR * NBR
     rows = atoms * NBR
     row = lax.broadcasted_iota(jnp.int32, (rows, atoms), 0)
     col = lax.broadcasted_iota(jnp.int32, (rows, atoms), 1)
     repeat = jnp.where(row // NBR == col, 1.0, 0.0).astype(BF16)
+    row = lax.broadcasted_iota(jnp.int32, (pairs, BLOCK), 0)
+    col = lax.broadcasted_iota(jnp.int32, (pairs, BLOCK), 1)
+    return repeat, jnp.where(row % NBR == col % NBR, 1.0, 0.0).astype(BF16)
+
+
+def basis_blocks(turned, repeat, fold):
+    rows = repeat.shape[0]
+    pairs = turned.shape[0]
     wide = dot_nt(repeat, turned)
     row = lax.broadcasted_iota(jnp.int32, (rows, pairs), 0)
     col = lax.broadcasted_iota(jnp.int32, (rows, pairs), 1)
     wide = jnp.where(row % NBR == col // NBR, wide, 0.0).astype(BF16)
-    row = lax.broadcasted_iota(jnp.int32, (pairs, BLOCK), 0)
-    col = lax.broadcasted_iota(jnp.int32, (pairs, BLOCK), 1)
-    tiled = dot(wide, jnp.where(row % NBR == col % NBR, 1.0, 0.0).astype(BF16))
+    tiled = dot(wide, fold)
     row = lax.broadcasted_iota(jnp.int32, (rows, BLOCK), 0)
     col = lax.broadcasted_iota(jnp.int32, (rows, BLOCK), 1)
     return jnp.where((row % BLOCK) // NBR == col // NBR, tiled, 0.0).astype(BF16)
@@ -71,15 +77,14 @@
     return owner
 
 
-def fill_slots(slots_ref, sources, partner_ref, count):
+def fill_slots(slots_ref, at, source_ref, partner_ref, count):
     owners = [owner_of(partner_ref[n], count) for n in range(count)]
     for d in range(slots_ref.shape[0]):
         pick = jnp.int32(0)
         for n in range(1, count):
             pick = jnp.where(owners[n] == d, n, pick)
         start = pl.multiple_of(pick * BLOCK, BLOCK)
-        for at, source_ref in enumerate(sources):
-            slots_ref[d, at * BLOCK : (at + 1) * BLOCK, :] = source_ref[pl.ds(start, BLOCK), :]
+        slots_ref[d, at * BLOCK : (at + 1) * BLOCK, :] = source_ref[pl.ds(start, BLOCK), :]
 
 
 def reversed_blocks(arrived_ref, sources, partner_ref, count):
@@ -120,8 +125,9 @@
     edge_copy.start()
     for copy in weight_copies + partner_copies:
         copy.start()
+    repeat, fold = basis_choices(rows // NBR)
     turned_copy.wait()
-    blocks_ref[...] = basis_blocks(turned_ref[...], rows // NBR)
+    blocks_ref[...] = basis_blocks(turned_ref[...], repeat, fold)
     edge_copy.wait()
     mixed = jnp.concatenate(
         [
@@ -139,24 +145,26 @@
     weight_copies[0].wait()
     preact = dot(normed, weight_ref[0])
     sigma = sigmoid(preact)
-    slope_one_ref[...] = silu_slope(preact, sigma)
-    first = mixed + preact * sigma
+    gated = preact * sigma
+    slope_one_ref[...] = silu_slope(gated, sigma)
+    first = mixed + gated
     inverse = inverse_norm(first)
     unit = first * inverse
     normed = unit.astype(BF16)
     unit_two_ref[...] = unit
     inverse_two_ref[...] = inverse
     normed_two_ref[...] = normed
-    weight_copies[1].wait()
+    for copy in [weight_copies[1], *partner_copies]:
+        copy.wait()
+    fill_slots(slots_ref, 1, cotangent_ref, partner_ref, count)
     preact = dot(normed, weight_ref[1])
     sigma = sigmoid(preact)
-    slope_two_ref[...] = silu_slope(preact, sigma)
-    second = first + preact * sigma
+    gated = preact * sigma
+    slope_two_ref[...] = silu_slope(gated, sigma)
+    second = first + gated
     second_ref[...] = second
     sent_ref[...] = second.astype(BF16)
-    for copy in partner_copies:
-        copy.wait()
-    fill_slots(slots_ref, (sent_ref, cotangent_ref), partner_ref, count)
+    fill_slots(slots_ref, 0, sent_ref, partner_ref, count)
     weight_copies[2].wait()
 
 
@@ -188,11 +196,12 @@
     normed = unit.astype(BF16)
     preact = dot(normed, weight_ref[2])
     sigma = sigmoid(preact)
-    edge_out_ref[...] = (summed[:rows] + preact[:rows] * sigma[:rows]).astype(BF16)
+    gated = preact * sigma
+    edge_out_ref[...] = (summed[:rows] + gated[:rows]).astype(BF16)
     copy = pltpu.make_async_copy(edge_out_ref, edge_out_hbm, sems.at[0])
     copy.start()
     grad_summed, grad_pre_three = layer_backward(
-        unit, inverse, silu_slope(preact, sigma), weight_ref[2], upstream
+        unit, inverse, silu_slope(gated, sigma), weight_ref[2], upstream
     )
     grad_second = grad_summed[:rows] + grad_summed[rows:].astype(BF16).astype(F32)
     grad_first, grad_pre_two = layer_backward(

time: 89.6 us -> 89.5 us (level)
  no operation moved by 1% of the time
where the time goes in v6:
time: 89.5 us; the launch traced here: 89.2 us
  blocking collectives  75.8 us (85%)
  Pallas kernels  9.01 us (10%)
  starting transfers between devices  1.92 us (2%)
  waiting for transfers between devices  1.2 us (1%)
    all_to_all x1, blocking collectives, summed_over(): lax.all_to_all(pieces, axis, split_axis=0, concat_axis=0, tiled=True)  25.4 us
    all_to_all x1, blocking collectives, local(): lax.all_to_all(sent, 'grp', split_axis=0, concat_axis=0, tiled=True)  21.4 us
    all_to_all x1, blocking collectives, local(): lax.all_to_all(pair, 'grp', split_axis=0, concat_axis=0, tiled=True)  15.3 us
    all_to_all x1, blocking collectives, local(): lax.all_to_all(line, 'blk_1', split_axis=0, concat_axis=0, tiled=True)  13.7 us
    pallas_call x6, Pallas kernels, call(): pl.pallas_call(body, name=name, in_specs=[smem] * len(scalars) + [anywher...  9.01 us
    ppermute x1, starting transfers between devices, local(): other = lax.ppermute(send, 'blk_2', swap)  1.92 us
  transfers between devices with their start and end apart: 1, of which 1 were waited for; matrix products, arithmetic and copies ran while one was open for 0% of the time, Pallas kernels for 1%

profile of v6, /device:TPU:2, one launch (start us, length us, event | category | flops | bytes accessed | tf_op | source)
XLA Modules:
  0.0 89.2 jit_solution(14230205768371627478)
XLA Ops:
  0.6 3.0 %forward.1 = (f32[384,512]{1,0:T(8,128)S(1)}, f32[384,1]{1,0:T(8,128)S(1)}, bf16[384,512]{1,0:T(8,128)(2,1)S(1)}, f32[384,512]{1,0:T(8,128)S(1)}, f32[384,512]{1...) custom-call(s32[3]{0:T(128)} %partner_hbm.1, ...), custom_call_target="tpu_custom_call" | custom-call | tf_op jit(solution)/shard_map/forward/pallas_call | solution.py:290
  3.6 21.4 %all_to_all.20.arrived_ref = bf16[4,256,512]{2,1,0:T(8,128)(2,1)S(1)} all-to-all(bf16[4,256,512]{2,1,0:T(8,128)(2,1)S(1)} %get-tuple-element.26), channel_id=1, replica_groups=mesh['grp'=4,'blk_0'=12,'blk_1'=8,'blk_2'=2] {'grp'}, dimensions={0} | all-to-all | bytes 2097152 | tf_op jit(solution)/shard_map/all_to_all | solution.py:323
  25.0 4.5 %backward.1 = (bf16[384,512]{1,0:T(8,128)(2,1)}, bf16[3,2,128,512]{3,2,1,0:T(8,128)(2,1)S(1)}, bf16[3,2,128,512]{3,2,1,0:T(8,128)(2,1)S(1)}, bf16[384,512]{1,0:T(8,128)(2,1)S(1)}) custom-call(s32[3]{0:T(128)S(1)} %get-tuple-element.23.partner_ref, f32[384,512]{1,0:T(8,128)S(1)} %get-tuple-element.24.second_ref, ...), custom_call_target="tpu_custom_call" | custom-call | tf_op jit(solution)/shard_map/backward/pallas_call | solution.py:290
  29.5 1.9 %collective-permute-start = (bf16[3,2,128,512]{3,2,1,0:T(8,128)(2,1)S(1)}, bf16[3,2,128,512]{3,2,1,0:T(8,128)(2,1)S(1)}, u32[]{:S(2)}, u32[]{:S(2)}) collective-permute-start(bf16[3,2,128,512]{3,2,1,0:T(8,128)(2,1)S(1)} %get-tuple-element.41), channel_id=1, source_target_pairs={{0,1},{1,0},{2,3},{3,2},{4,5},{5,4},{6,7},{7,6},{8,9},{9,8},{10,11... | collective-permute-start | bytes 2359304 | tf_op jit(solution)/shard_map/ppermute | solution.py:333
  31.5 1.0 %finish.1 = (bf16[384,512]{1,0:T(8,128)(2,1)}, f32[8,128]{1,0:T(8,128)S(1)}) custom-call(bf16[384,512]{1,0:T(8,128)(2,1)S(1)} %get-tuple-element.37.grad_round_ref, bf16[384,128]{1,0:T(8,128)(2,1)S(1)} %get-tuple-element.38.blocks_ref), custom_call_target="tpu_custom_call" | custom-call | tf_op jit(solution)/shard_map/finish/pallas_call | solution.py:290
  32.5 1.2 %collective-permute-done.other_ref = bf16[3,2,128,512]{3,2,1,0:T(8,128)(2,1)S(1)} collective-permute-done((bf16[3,2,128,512]{3,2,1,0:T(8,128)(2,1)S(1)}, bf16[3,2,128,512]{3,2,1,0:T(8,128)(2,1)S(1)}, u32[]{:S(2)}, u32[]{:S(2)}) %collective-permute-start) | collective-permute-done | bytes 786464 | tf_op jit(solution)/shard_map/ppermute | solution.py:333
  33.7 0.2 join.1
  33.9 15.3 %all_to_all.21.arrived_ref = bf16[4,2,96,512]{3,2,1,0:T(8,128)(2,1)S(1)} all-to-all(bf16[4,2,96,512]{3,2,1,0:T(8,128)(2,1)S(1)} %join.1), channel_id=1, replica_groups=mesh['grp'=4,'blk_0'=12,'blk_1'=8,'blk_2'=2] {'grp'}, dimensions={0} | all-to-all | bytes 1572864 | tf_op jit(solution)/shard_map/all_to_all | solution.py:342
  49.2 0.3 line.1
  49.4 13.7 %all_to_all.22.column_ref = bf16[8,24,512]{2,1,0:T(8,128)(2,1)S(1)} all-to-all(bf16[8,24,512]{2,1,0:T(8,128)(2,1)S(1)} %line.1), channel_id=1, replica_groups=mesh['grp'=4,'blk_0'=12,'blk_1'=8,'blk_2'=2] {'blk_1'}, dimensions={0} | all-to-all | bytes 393216 | tf_op jit(solution)/shard_map/all_to_all | solution.py:348
  63.2 25.4 %all_to_all.23 = bf16[12,2,512]{2,1,0:T(2,128)(2,1)S(1)} all-to-all(bf16[12,2,512]{2,1,0:T(2,128)(2,1)S(1)} %plane.1), channel_id=1, replica_groups=mesh['grp'=4,'blk_0'=12,'blk_1'=8,'blk_2'=2] {'blk_0'}, dimensions={0} | all-to-all | bytes 49152 | tf_op jit(solution)/shard_map/all_to_all | solution.py:302
  88.6 0.6 broadcast_multiply_fusion
  (2 shorter events, 0.1 us)
Async XLA Ops:
  29.5 4.2 %collective-permute-start = (bf16[3,2,128,512]{3,2,1,0:T(8,128)(2,1)S(1)}, bf16[3,2,128,512]{3,2,1,0:T(8,128)(2,1)S(1)}, u32[]{:S(2)}, u32[]{:S(2)}) collective-permute-start(bf16[3,2,128,512]{3,2,1,0:T(8,128)(2,1)S(1)} %get-tuple-element.41), channel_id=1, source_target_pairs={{0,1},{1,0},{2,3},{3,2},{4,5},{5,4},{6,7},{7,6},{8,9},{9,8},{10,11... | collective-permute-start | bytes 2359304 | tf_op jit(solution)/shard_map/ppermute | solution.py:333
